TPU v7x, 512 devices: a whole 4x8x8 slice. The times are simulated.
512 devices in a mesh: section: 32 (over y_hi, z, core), dp: 16 (over x, y_lo).
Axes of the slice: x: 4, y: 8 (y_hi: 2, y_lo: 4; y = y_hi * 4 + y_lo), z: 8, core: 2. Of those that a mesh axis runs over, the one named last changes fastest.
Arguments:
- section_inputs: bfloat16 [32, 2048, 4096], P('section', 'dp'), may hold values from -6 to 6
- norm_gain: bfloat16 [32, 4096], P('section'), may hold values from 0.5 to 1.5
- down_proj: bfloat16 [32, 4096, 256], P('section', 'dp'), may hold values from -0.09375 to 0.09375
- up_proj: bfloat16 [32, 256, 4096], P('section', None, 'dp'), may hold values from -0.1875 to 0.1875
- readout_matrix: bfloat16 [4096, 128], P('dp'), may hold values from -0.09375 to 0.09375
- ground_truth_series: float32 [2048, 128], P('dp'), may hold values from -6 to 6
- valid_len: int32 [128], P('dp'), may hold values from 1 to 16
Outputs:
- input_grads: bfloat16 [32, 2048, 4096], P('section', 'dp')
- down_grads: bfloat16 [32, 4096, 256], P('section', 'dp')
- up_grads: bfloat16 [32, 256, 4096], P('section', None, 'dp')
All inputs are finite; a program needn't handle non-finite values.
Results may differ from a plain program's by a relative error of at most 0.035.
Values may be sent and summed in bfloat16 or wider, within the bound.
A program may use at most 64 MiB of HBM per device.

v0:
```python
import jax
import jax.numpy as jnp
from jax import lax
from jax.sharding import PartitionSpec as P

EPSILON = 1e-05


def from_behind(block, axis, distance):
    devices = range(lax.axis_size(axis))
    route = [(i - distance, i) for i in devices if i - distance in devices]
    return lax.ppermute(block, axis, route)


def normalize(inputs, gain_row):
    values = inputs.astype(jnp.float32)
    inverse = lax.rsqrt(jnp.mean(values * values, axis=-1, keepdims=True) + EPSILON)
    unit = values * inverse
    normed = (unit * gain_row.astype(jnp.float32)).astype(jnp.bfloat16)
    return (inverse, unit, normed)


def multiply_trailing_factor(left, right):
    return lax.dot_general(
        left, right, (((1,), (1,)), ((), ())), preferred_element_type=jnp.float32
    )


def contract_rows(left, right):
    return lax.dot_general(
        left, right, (((0,), (0,)), ((), ())), preferred_element_type=jnp.float32
    )


def block_backward(inverse, unit, latent, gain_row, down_full, up_full, arriving_gradient):
    sigmoid = jax.nn.sigmoid(latent)
    hidden_grad = multiply_trailing_factor(arriving_gradient, up_full)
    latent_grad = (hidden_grad * sigmoid * (1.0 + latent * (1.0 - sigmoid))).astype(jnp.bfloat16)
    scaled = multiply_trailing_factor(latent_grad, down_full) * gain_row.astype(jnp.float32)
    inputs_grad = arriving_gradient.astype(jnp.float32) + inverse * (
        scaled - unit * jnp.mean(scaled * unit, axis=-1, keepdims=True)
    )
    return (inputs_grad.astype(jnp.bfloat16), latent_grad)


def per_device(
    section_inputs, norm_gain, down_proj, up_proj, readout_matrix, ground_truth_series, valid_len
):
    down_full, up_full, entire_readout_matrix = (
        lax.all_gather(down_proj[0], "dp", axis=0, tiled=True),
        lax.all_gather(up_proj[0], "dp", axis=1, tiled=True),
        lax.all_gather(readout_matrix, "dp", axis=0, tiled=True),
    )
    inputs = section_inputs[0]
    gain_row = norm_gain[0]
    microbatch_count = valid_len.shape[0]
    token_count = inputs.shape[0]
    row_count = token_count // microbatch_count
    width = inputs.shape[1]
    latent_width = down_full.shape[1]
    inverse, unit, normed = normalize(inputs, gain_row)
    latent = jnp.dot(normed, down_full, preferred_element_type=jnp.float32)
    activated = jax.nn.silu(latent).astype(jnp.bfloat16)
    section_index = lax.axis_index("section")
    section_last = lax.axis_size("section") - 1
    observed_entry_indicator = (
        (jnp.arange(row_count)[None, :] < valid_len[:, None])
        .astype(jnp.float32)
        .reshape(token_count)
    )

    def loss_grad(unused):
        adapter_output = (
            inputs.astype(jnp.float32)
            + jnp.dot(activated, up_full, preferred_element_type=jnp.float32)
        ).astype(jnp.bfloat16)
        estimated_horizon = jnp.dot(
            adapter_output, entire_readout_matrix, preferred_element_type=jnp.float32
        )
        prediction_discrepancy = (
            observed_entry_indicator[:, None] * (estimated_horizon - ground_truth_series)
        ).astype(jnp.bfloat16)
        return multiply_trailing_factor(prediction_discrepancy, entire_readout_matrix).astype(
            jnp.bfloat16
        )

    def no_loss(unused):
        return jnp.zeros((token_count, width), jnp.bfloat16)

    top_grads = lax.cond(section_index == section_last, loss_grad, no_loss, 0).reshape(
        microbatch_count, row_count, width
    )
    inverse_micro = inverse.reshape(microbatch_count, row_count, 1)
    unit_micro = unit.reshape(microbatch_count, row_count, width)
    latent_micro = latent.reshape(microbatch_count, row_count, latent_width)

    def tick(tick_num, carry):
        outgoing, grads_in, latent_grads, cotangents = carry
        received = from_behind(outgoing, "section", -1)
        micro_num = tick_num - (section_last - section_index)
        is_valid = (micro_num >= 0) & (micro_num < microbatch_count)
        picked = jnp.clip(micro_num, 0, microbatch_count - 1)

        def process(state):
            arrived, grads_prev, latent_prev, cotangent_prev = state
            top_piece = lax.dynamic_index_in_dim(top_grads, picked, 0, keepdims=False)
            arriving_gradient = jnp.where(section_index == section_last, top_piece, arrived)
            inputs_grad, latent_grad = block_backward(
                lax.dynamic_index_in_dim(inverse_micro, picked, 0, keepdims=False),
                lax.dynamic_index_in_dim(unit_micro, picked, 0, keepdims=False),
                lax.dynamic_index_in_dim(latent_micro, picked, 0, keepdims=False),
                gain_row,
                down_full,
                up_full,
                arriving_gradient,
            )
            grads_next = lax.dynamic_update_index_in_dim(grads_prev, inputs_grad, picked, 0)
            latent_next = lax.dynamic_update_index_in_dim(latent_prev, latent_grad, picked, 0)
            cotangent_next = lax.dynamic_update_index_in_dim(
                cotangent_prev, arriving_gradient, picked, 0
            )
            return (inputs_grad, grads_next, latent_next, cotangent_next)

        def skipped(state):
            return state

        return lax.cond(is_valid, process, skipped, (received, grads_in, latent_grads, cotangents))

    initial = (
        jnp.zeros((row_count, width), jnp.bfloat16),
        jnp.zeros((microbatch_count, row_count, width), jnp.bfloat16),
        jnp.zeros((microbatch_count, row_count, latent_width), jnp.bfloat16),
        jnp.zeros((microbatch_count, row_count, width), jnp.bfloat16),
    )
    tick_total = lax.axis_size("section") + microbatch_count - 1
    final_state = lax.fori_loop(0, tick_total, tick, initial)
    grads_in = final_state[1].reshape(1, token_count, width)
    latent_grads = final_state[2].reshape(token_count, latent_width)
    cotangents = final_state[3].reshape(token_count, width)
    down_sum = lax.psum_scatter(
        contract_rows(normed, latent_grads), "dp", scatter_dimension=0, tiled=True
    )
    activated_all = lax.all_gather(activated, "dp", axis=0, tiled=True)
    cotangent_cols = lax.all_to_all(cotangents, "dp", split_axis=1, concat_axis=0, tiled=True)
    up_sum = contract_rows(activated_all, cotangent_cols)
    down_grads = down_sum.astype(jnp.bfloat16)[None]
    up_grads = up_sum.astype(jnp.bfloat16)[None]
    return (grads_in, down_grads, up_grads)


def solution(mesh):
    placed = (
        P("section", "dp", None),
        P("section", None),
        P("section", "dp", None),
        P("section", None, "dp"),
        P("dp", None),
        P("dp", None),
        P("dp"),
    )
    return jax.shard_map(
        per_device,
        mesh=mesh,
        in_specs=placed,
        out_specs=(P("section", "dp", None), P("section", "dp", None), P("section", None, "dp")),
        check_vma=False,
    )
```

profile of v0, /device:TPU:448, one launch (start us, length us, event | category | flops | bytes accessed | tf_op | source)
XLA Modules:
  0.0 932.3 jit_solution(12533757512585029941)
XLA Ops:
  11.8 87.0 %all-gather.11.cloned.1.call-done = bf16[1,4096,256]{2,1,0:T(8,128)(2,1)} async-done(((bf16[1,256,256]{2,1,0:T(8,128)(2,1)}), bf16[1,4096,256]{2,1,0:T(8,128)(2,1)}) %all-gather.11.cloned.1.call-update) | async-done | bytes 2097168 | tf_op jit(solution)/shard_map/all_gather | solution.py:50
  98.8 3.1 multiply_convert_fusion.1
  103.7 80.8 %all-gather.7.cloned.1.call-done = bf16[4096,128]{1,0:T(8,128)(2,1)} async-done(((bf16[256,128]{1,0:T(8,128)(2,1)}), bf16[4096,128]{1,0:T(8,128)(2,1)}) %all-gather.7.cloned.1.call-update) | async-done | bytes 1048592 | tf_op jit(solution)/shard_map/all_gather | solution.py:52
  184.5 87.1 %all-gather.13.cloned.1.call-done = bf16[1,256,4096]{2,1,0:T(8,128)(2,1)} async-done(((bf16[1,256,256]{2,1,0:T(8,128)(2,1)}), bf16[1,256,4096]{2,1,0:T(8,128)(2,1)}) %all-gather.13.cloned.1.call-update) | async-done | bytes 2097168 | tf_op jit(solution)/shard_map/all_gather | solution.py:51
  275.1 521.3 %while.20 = (s32[]{:T(128)}, bf16[16,4096]{1,0:T(8,128)(2,1)S(1)}, bf16[8,16,4096]{2,1,0:T(8,128)(2,1)}, bf16[8,16,256]{2,1,0:T(8,128)(2,1)S(1)}, bf16[8,16,4096...) while((s32[]{:T(128)}, bf16[16,4096]{1,0:T(8,128)(2,1)S(1)}, ...), condition=%wide.region_7.8_spmd, body=%wide.region_3.7_spmd.sunk | while | flops 67805192 | bytes 15549357 | solution.py:136
  277.1 2.5 collective-permute-done
  279.6 3.8 collective-permute-start
  283.4 2.5 collective-permute-done
  285.9 3.8 collective-permute-start
  289.7 7.3 collective-permute-done
  299.0 10.7 %collective-permute-done = bf16[16,4096]{1,0:T(8,128)(2,1)S(1)} collective-permute-done((bf16[16,4096]{1,0:T(8,128)(2,1)S(1)}, bf16[16,4096]{1,0:T(8,128)(2,1)S(1)}, u32[]{:S(2)}, u32[]{:S(2)}) %collective-permute-start) | collective-permute-done | bytes 131104 | tf_op jit(solution)/shard_map/while/body/eval_jaxpr/ppermute | solution.py:12
  311.6 10.6 %collective-permute-done = bf16[16,4096]{1,0:T(8,128)(2,1)S(1)} collective-permute-done((bf16[16,4096]{1,0:T(8,128)(2,1)S(1)}, bf16[16,4096]{1,0:T(8,128)(2,1)S(1)}, u32[]{:S(2)}, u32[]{:S(2)}) %collective-permute-start) | collective-permute-done | bytes 131104 | tf_op jit(solution)/shard_map/while/body/eval_jaxpr/ppermute | solution.py:12
  322.2 1.9 collective-permute-start
  324.2 10.9 %collective-permute-done = bf16[16,4096]{1,0:T(8,128)(2,1)S(1)} collective-permute-done((bf16[16,4096]{1,0:T(8,128)(2,1)S(1)}, bf16[16,4096]{1,0:T(8,128)(2,1)S(1)}, u32[]{:S(2)}, u32[]{:S(2)}) %collective-permute-start) | collective-permute-done | bytes 131104 | tf_op jit(solution)/shard_map/while/body/eval_jaxpr/ppermute | solution.py:12
  335.1 1.9 collective-permute-start
  337.0 11.3 %collective-permute-done = bf16[16,4096]{1,0:T(8,128)(2,1)S(1)} collective-permute-done((bf16[16,4096]{1,0:T(8,128)(2,1)S(1)}, bf16[16,4096]{1,0:T(8,128)(2,1)S(1)}, u32[]{:S(2)}, u32[]{:S(2)}) %collective-permute-start) | collective-permute-done | bytes 131104 | tf_op jit(solution)/shard_map/while/body/eval_jaxpr/ppermute | solution.py:12
  348.4 1.9 collective-permute-start
  350.3 10.7 %collective-permute-done = bf16[16,4096]{1,0:T(8,128)(2,1)S(1)} collective-permute-done((bf16[16,4096]{1,0:T(8,128)(2,1)S(1)}, bf16[16,4096]{1,0:T(8,128)(2,1)S(1)}, u32[]{:S(2)}, u32[]{:S(2)}) %collective-permute-start) | collective-permute-done | bytes 131104 | tf_op jit(solution)/shard_map/while/body/eval_jaxpr/ppermute | solution.py:12
  363.0 10.4 %collective-permute-done = bf16[16,4096]{1,0:T(8,128)(2,1)S(1)} collective-permute-done((bf16[16,4096]{1,0:T(8,128)(2,1)S(1)}, bf16[16,4096]{1,0:T(8,128)(2,1)S(1)}, u32[]{:S(2)}, u32[]{:S(2)}) %collective-permute-start) | collective-permute-done | bytes 131104 | tf_op jit(solution)/shard_map/while/body/eval_jaxpr/ppermute | solution.py:12
  375.4 10.4 %collective-permute-done = bf16[16,4096]{1,0:T(8,128)(2,1)S(1)} collective-permute-done((bf16[16,4096]{1,0:T(8,128)(2,1)S(1)}, bf16[16,4096]{1,0:T(8,128)(2,1)S(1)}, u32[]{:S(2)}, u32[]{:S(2)}) %collective-permute-start) | collective-permute-done | bytes 131104 | tf_op jit(solution)/shard_map/while/body/eval_jaxpr/ppermute | solution.py:12
  385.8 1.9 collective-permute-start
  387.7 10.4 %collective-permute-done = bf16[16,4096]{1,0:T(8,128)(2,1)S(1)} collective-permute-done((bf16[16,4096]{1,0:T(8,128)(2,1)S(1)}, bf16[16,4096]{1,0:T(8,128)(2,1)S(1)}, u32[]{:S(2)}, u32[]{:S(2)}) %collective-permute-start) | collective-permute-done | bytes 131104 | tf_op jit(solution)/shard_map/while/body/eval_jaxpr/ppermute | solution.py:12
  400.0 10.4 %collective-permute-done = bf16[16,4096]{1,0:T(8,128)(2,1)S(1)} collective-permute-done((bf16[16,4096]{1,0:T(8,128)(2,1)S(1)}, bf16[16,4096]{1,0:T(8,128)(2,1)S(1)}, u32[]{:S(2)}, u32[]{:S(2)}) %collective-permute-start) | collective-permute-done | bytes 131104 | tf_op jit(solution)/shard_map/while/body/eval_jaxpr/ppermute | solution.py:12
  412.4 10.4 %collective-permute-done = bf16[16,4096]{1,0:T(8,128)(2,1)S(1)} collective-permute-done((bf16[16,4096]{1,0:T(8,128)(2,1)S(1)}, bf16[16,4096]{1,0:T(8,128)(2,1)S(1)}, u32[]{:S(2)}, u32[]{:S(2)}) %collective-permute-start) | collective-permute-done | bytes 131104 | tf_op jit(solution)/shard_map/while/body/eval_jaxpr/ppermute | solution.py:12
  424.7 10.4 %collective-permute-done = bf16[16,4096]{1,0:T(8,128)(2,1)S(1)} collective-permute-done((bf16[16,4096]{1,0:T(8,128)(2,1)S(1)}, bf16[16,4096]{1,0:T(8,128)(2,1)S(1)}, u32[]{:S(2)}, u32[]{:S(2)}) %collective-permute-start) | collective-permute-done | bytes 131104 | tf_op jit(solution)/shard_map/while/body/eval_jaxpr/ppermute | solution.py:12
  437.0 10.4 %collective-permute-done = bf16[16,4096]{1,0:T(8,128)(2,1)S(1)} collective-permute-done((bf16[16,4096]{1,0:T(8,128)(2,1)S(1)}, bf16[16,4096]{1,0:T(8,128)(2,1)S(1)}, u32[]{:S(2)}, u32[]{:S(2)}) %collective-permute-start) | collective-permute-done | bytes 131104 | tf_op jit(solution)/shard_map/while/body/eval_jaxpr/ppermute | solution.py:12
  449.4 10.4 %collective-permute-done = bf16[16,4096]{1,0:T(8,128)(2,1)S(1)} collective-permute-done((bf16[16,4096]{1,0:T(8,128)(2,1)S(1)}, bf16[16,4096]{1,0:T(8,128)(2,1)S(1)}, u32[]{:S(2)}, u32[]{:S(2)}) %collective-permute-start) | collective-permute-done | bytes 131104 | tf_op jit(solution)/shard_map/while/body/eval_jaxpr/ppermute | solution.py:12
  461.7 10.4 %collective-permute-done = bf16[16,4096]{1,0:T(8,128)(2,1)S(1)} collective-permute-done((bf16[16,4096]{1,0:T(8,128)(2,1)S(1)}, bf16[16,4096]{1,0:T(8,128)(2,1)S(1)}, u32[]{:S(2)}, u32[]{:S(2)}) %collective-permute-start) | collective-permute-done | bytes 131104 | tf_op jit(solution)/shard_map/while/body/eval_jaxpr/ppermute | solution.py:12
  474.0 17.0 %collective-permute-done = bf16[16,4096]{1,0:T(8,128)(2,1)S(1)} collective-permute-done((bf16[16,4096]{1,0:T(8,128)(2,1)S(1)}, bf16[16,4096]{1,0:T(8,128)(2,1)S(1)}, u32[]{:S(2)}, u32[]{:S(2)}) %collective-permute-start) | collective-permute-done | bytes 131104 | tf_op jit(solution)/shard_map/while/body/eval_jaxpr/ppermute | solution.py:12
  491.0 6.6 conditional.4
  499.6 10.4 %collective-permute-done = bf16[16,4096]{1,0:T(8,128)(2,1)S(1)} collective-permute-done((bf16[16,4096]{1,0:T(8,128)(2,1)S(1)}, bf16[16,4096]{1,0:T(8,128)(2,1)S(1)}, u32[]{:S(2)}, u32[]{:S(2)}) %collective-permute-start) | collective-permute-done | bytes 131104 | tf_op jit(solution)/shard_map/while/body/eval_jaxpr/ppermute | solution.py:12
  510.0 6.6 conditional.4
  518.5 10.4 %collective-permute-done = bf16[16,4096]{1,0:T(8,128)(2,1)S(1)} collective-permute-done((bf16[16,4096]{1,0:T(8,128)(2,1)S(1)}, bf16[16,4096]{1,0:T(8,128)(2,1)S(1)}, u32[]{:S(2)}, u32[]{:S(2)}) %collective-permute-start) | collective-permute-done | bytes 131104 | tf_op jit(solution)/shard_map/while/body/eval_jaxpr/ppermute | solution.py:12
  528.9 6.6 conditional.4
  537.5 10.4 %collective-permute-done = bf16[16,4096]{1,0:T(8,128)(2,1)S(1)} collective-permute-done((bf16[16,4096]{1,0:T(8,128)(2,1)S(1)}, bf16[16,4096]{1,0:T(8,128)(2,1)S(1)}, u32[]{:S(2)}, u32[]{:S(2)}) %collective-permute-start) | collective-permute-done | bytes 131104 | tf_op jit(solution)/shard_map/while/body/eval_jaxpr/ppermute | solution.py:12
  547.8 6.6 conditional.4
  556.4 10.4 %collective-permute-done = bf16[16,4096]{1,0:T(8,128)(2,1)S(1)} collective-permute-done((bf16[16,4096]{1,0:T(8,128)(2,1)S(1)}, bf16[16,4096]{1,0:T(8,128)(2,1)S(1)}, u32[]{:S(2)}, u32[]{:S(2)}) %collective-permute-start) | collective-permute-done | bytes 131104 | tf_op jit(solution)/shard_map/while/body/eval_jaxpr/ppermute | solution.py:12
  566.8 6.6 conditional.4
  575.4 10.3 %collective-permute-done = bf16[16,4096]{1,0:T(8,128)(2,1)S(1)} collective-permute-done((bf16[16,4096]{1,0:T(8,128)(2,1)S(1)}, bf16[16,4096]{1,0:T(8,128)(2,1)S(1)}, u32[]{:S(2)}, u32[]{:S(2)}) %collective-permute-start) | collective-permute-done | bytes 131104 | tf_op jit(solution)/shard_map/while/body/eval_jaxpr/ppermute | solution.py:12
  585.8 6.6 conditional.4
  594.4 10.3 %collective-permute-done = bf16[16,4096]{1,0:T(8,128)(2,1)S(1)} collective-permute-done((bf16[16,4096]{1,0:T(8,128)(2,1)S(1)}, bf16[16,4096]{1,0:T(8,128)(2,1)S(1)}, u32[]{:S(2)}, u32[]{:S(2)}) %collective-permute-start) | collective-permute-done | bytes 131104 | tf_op jit(solution)/shard_map/while/body/eval_jaxpr/ppermute | solution.py:12
  604.7 6.6 conditional.4
  613.3 10.4 %collective-permute-done = bf16[16,4096]{1,0:T(8,128)(2,1)S(1)} collective-permute-done((bf16[16,4096]{1,0:T(8,128)(2,1)S(1)}, bf16[16,4096]{1,0:T(8,128)(2,1)S(1)}, u32[]{:S(2)}, u32[]{:S(2)}) %collective-permute-start) | collective-permute-done | bytes 131104 | tf_op jit(solution)/shard_map/while/body/eval_jaxpr/ppermute | solution.py:12
  623.7 6.6 conditional.4
  632.2 3.8 collective-permute-done
  636.0 9.1 collective-permute-start
  645.2 3.2 collective-permute-done
  648.4 3.1 collective-permute-start
  651.5 9.2 collective-permute-done
  662.6 10.4 %collective-permute-done = bf16[16,4096]{1,0:T(8,128)(2,1)S(1)} collective-permute-done((bf16[16,4096]{1,0:T(8,128)(2,1)S(1)}, bf16[16,4096]{1,0:T(8,128)(2,1)S(1)}, u32[]{:S(2)}, u32[]{:S(2)}) %collective-permute-start) | collective-permute-done | bytes 131104 | tf_op jit(solution)/shard_map/while/body/eval_jaxpr/ppermute | solution.py:12
  675.0 10.4 %collective-permute-done = bf16[16,4096]{1,0:T(8,128)(2,1)S(1)} collective-permute-done((bf16[16,4096]{1,0:T(8,128)(2,1)S(1)}, bf16[16,4096]{1,0:T(8,128)(2,1)S(1)}, u32[]{:S(2)}, u32[]{:S(2)}) %collective-permute-start) | collective-permute-done | bytes 131104 | tf_op jit(solution)/shard_map/while/body/eval_jaxpr/ppermute | solution.py:12
  687.3 10.4 %collective-permute-done = bf16[16,4096]{1,0:T(8,128)(2,1)S(1)} collective-permute-done((bf16[16,4096]{1,0:T(8,128)(2,1)S(1)}, bf16[16,4096]{1,0:T(8,128)(2,1)S(1)}, u32[]{:S(2)}, u32[]{:S(2)}) %collective-permute-start) | collective-permute-done | bytes 131104 | tf_op jit(solution)/shard_map/while/body/eval_jaxpr/ppermute | solution.py:12
  699.6 10.4 %collective-permute-done = bf16[16,4096]{1,0:T(8,128)(2,1)S(1)} collective-permute-done((bf16[16,4096]{1,0:T(8,128)(2,1)S(1)}, bf16[16,4096]{1,0:T(8,128)(2,1)S(1)}, u32[]{:S(2)}, u32[]{:S(2)}) %collective-permute-start) | collective-permute-done | bytes 131104 | tf_op jit(solution)/shard_map/while/body/eval_jaxpr/ppermute | solution.py:12
  712.0 10.4 %collective-permute-done = bf16[16,4096]{1,0:T(8,128)(2,1)S(1)} collective-permute-done((bf16[16,4096]{1,0:T(8,128)(2,1)S(1)}, bf16[16,4096]{1,0:T(8,128)(2,1)S(1)}, u32[]{:S(2)}, u32[]{:S(2)}) %collective-permute-start) | collective-permute-done | bytes 131104 | tf_op jit(solution)/shard_map/while/body/eval_jaxpr/ppermute | solution.py:12
  724.3 10.4 %collective-permute-done = bf16[16,4096]{1,0:T(8,128)(2,1)S(1)} collective-permute-done((bf16[16,4096]{1,0:T(8,128)(2,1)S(1)}, bf16[16,4096]{1,0:T(8,128)(2,1)S(1)}, u32[]{:S(2)}, u32[]{:S(2)}) %collective-permute-start) | collective-permute-done | bytes 131104 | tf_op jit(solution)/shard_map/while/body/eval_jaxpr/ppermute | solution.py:12
  736.6 10.4 %collective-permute-done = bf16[16,4096]{1,0:T(8,128)(2,1)S(1)} collective-permute-done((bf16[16,4096]{1,0:T(8,128)(2,1)S(1)}, bf16[16,4096]{1,0:T(8,128)(2,1)S(1)}, u32[]{:S(2)}, u32[]{:S(2)}) %collective-permute-start) | collective-permute-done | bytes 131104 | tf_op jit(solution)/shard_map/while/body/eval_jaxpr/ppermute | solution.py:12
  749.0 10.4 %collective-permute-done = bf16[16,4096]{1,0:T(8,128)(2,1)S(1)} collective-permute-done((bf16[16,4096]{1,0:T(8,128)(2,1)S(1)}, bf16[16,4096]{1,0:T(8,128)(2,1)S(1)}, u32[]{:S(2)}, u32[]{:S(2)}) %collective-permute-start) | collective-permute-done | bytes 131104 | tf_op jit(solution)/shard_map/while/body/eval_jaxpr/ppermute | solution.py:12
  761.3 10.4 %collective-permute-done = bf16[16,4096]{1,0:T(8,128)(2,1)S(1)} collective-permute-done((bf16[16,4096]{1,0:T(8,128)(2,1)S(1)}, bf16[16,4096]{1,0:T(8,128)(2,1)S(1)}, u32[]{:S(2)}, u32[]{:S(2)}) %collective-permute-start) | collective-permute-done | bytes 131104 | tf_op jit(solution)/shard_map/while/body/eval_jaxpr/ppermute | solution.py:12
  773.6 10.4 %collective-permute-done = bf16[16,4096]{1,0:T(8,128)(2,1)S(1)} collective-permute-done((bf16[16,4096]{1,0:T(8,128)(2,1)S(1)}, bf16[16,4096]{1,0:T(8,128)(2,1)S(1)}, u32[]{:S(2)}, u32[]{:S(2)}) %collective-permute-start) | collective-permute-done | bytes 131104 | tf_op jit(solution)/shard_map/while/body/eval_jaxpr/ppermute | solution.py:12
  786.0 10.4 %collective-permute-done = bf16[16,4096]{1,0:T(8,128)(2,1)S(1)} collective-permute-done((bf16[16,4096]{1,0:T(8,128)(2,1)S(1)}, bf16[16,4096]{1,0:T(8,128)(2,1)S(1)}, u32[]{:S(2)}, u32[]{:S(2)}) %collective-permute-start) | collective-permute-done | bytes 131104 | tf_op jit(solution)/shard_map/while/body/eval_jaxpr/ppermute | solution.py:12
  796.4 2.8 fusion.22
  801.0 43.8 %all_to_all.19 = bf16[128,16,256]{2,0,1:T(8,128)(2,1)S(1)} all-to-all(bf16[128,16,256]{2,0,1:T(8,128)(2,1)S(1)} %copy.16), channel_id=1, replica_groups=mesh['section'=32,'dp'=16] {'dp'}, dimensions={1} | all-to-all | bytes 2097152 | tf_op jit(solution)/shard_map/all_to_all | solution.py:144
  844.7 2.4 fusion.20
  847.1 77.1 %reduce-scatter.2.cloned.1.call-done = f32[256,256]{1,0:T(8,128)} async-done(((f32[4096,256]{1,0:T(8,128)}), f32[256,256]{1,0:T(8,128)}) %reduce-scatter.2.cloned.1.call-update) | async-done | bytes 262160 | tf_op jit(solution)/shard_map/reduce_scatter | solution.py:140
  (213 shorter events, 126.9 us)
Async XLA Ops:
  7.2 91.6 %all-gather.11.cloned.1.call-start = ((), (), s32[]{:S(2)}) async-start(), calls=%async_computation.5 | async-start | bytes 2228224 | tf_op jit(solution)/shard_map/all_gather | solution.py:50
  7.9 176.6 %all-gather.7.cloned.1.call-start = ((), (), s32[]{:S(2)}) async-start(), calls=%async_computation.2 | async-start | bytes 1114112 | tf_op jit(solution)/shard_map/all_gather | solution.py:52
  8.6 263.0 %all-gather.13.cloned.1.call-start = ((), (), s32[]{:S(2)}) async-start(), calls=%async_computation.6 | async-start | bytes 2228224 | tf_op jit(solution)/shard_map/all_gather | solution.py:51
  9.4 835.3 %all-gather.9.cloned.1.call-start = ((), (), s32[]{:S(2)}) async-start(), calls=%async_computation.4 | async-start | bytes 1114112 | tf_op jit(solution)/shard_map/all_gather | solution.py:143
  11.7 90.4 %copy-start.7 = (s32[8]{0:T(128)S(1)}, s32[8]{0:T(128)}, u32[]{:S(2)}) copy-start(s32[8]{0:T(128)} %param.19) | copy-start | bytes 100
  11.7 90.4 %copy-start.2 = (bf16[1,128,4096]{2,1,0:T(8,128)(2,1)S(1)}, bf16[1,128,4096]{2,1,0:T(8,128)(2,1)}, u32[]{:S(2)}) copy-start(bf16[1,128,4096]{2,1,0:T(8,128)(2,1)} %param.13) | copy-start | bytes 3145732
  101.9 169.8 %copy-start.5 = (bf16[128,256]{1,0:T(8,128)(2,1)S(1)}, bf16[128,256]{1,0:T(8,128)(2,1)}, u32[]{:S(2)}) copy-start(bf16[128,256]{1,0:T(8,128)(2,1)} %get-tuple-element.490) | copy-start | bytes 196612
  101.9 169.8 %copy-start.6 = (f32[128,128]{1,0:T(8,128)S(1)}, f32[128,128]{1,0:T(8,128)}, u32[]{:S(2)}) copy-start(f32[128,128]{1,0:T(8,128)} %param.18) | copy-start | bytes 196612
  101.9 822.3 %reduce-scatter.2.cloned.1.call-start = ((), (), s32[]{:S(2)}) async-start(), calls=%async_computation.3 | async-start | bytes 4456448 | tf_op jit(solution)/shard_map/reduce_scatter | solution.py:140
  272.8 2.3 copy-start
  275.1 4.4 collective-permute-start
  279.6 6.3 collective-permute-start
  285.9 11.1 %collective-permute-start = (bf16[16,4096]{1,0:T(8,128)(2,1)S(1)}, bf16[16,4096]{1,0:T(8,128)(2,1)S(1)}, u32[]{:S(2)}, u32[]{:S(2)}) collective-permute-start(bf16[16,4096]{1,0:T(8,128)(2,1)S(1)} %get-tuple-element.611), channel_id=1, source_target_pairs={{16,0},{32,16},{48,32},{64,48},{80,64},{96,80},{112,96},{128,112},... | collective-permute-start | bytes 393224 | tf_op jit(solution)/shard_map/while/body/eval_jaxpr/ppermute | solution.py:12
  297.0 12.7 %collective-permute-start = (bf16[16,4096]{1,0:T(8,128)(2,1)S(1)}, bf16[16,4096]{1,0:T(8,128)(2,1)S(1)}, u32[]{:S(2)}, u32[]{:S(2)}) collective-permute-start(bf16[16,4096]{1,0:T(8,128)(2,1)S(1)} %get-tuple-element.611), channel_id=1, source_target_pairs={{16,0},{32,16},{48,32},{64,48},{80,64},{96,80},{112,96},{128,112},... | collective-permute-start | bytes 393224 | tf_op jit(solution)/shard_map/while/body/eval_jaxpr/ppermute | solution.py:12
  309.7 12.5 %collective-permute-start = (bf16[16,4096]{1,0:T(8,128)(2,1)S(1)}, bf16[16,4096]{1,0:T(8,128)(2,1)S(1)}, u32[]{:S(2)}, u32[]{:S(2)}) collective-permute-start(bf16[16,4096]{1,0:T(8,128)(2,1)S(1)} %get-tuple-element.611), channel_id=1, source_target_pairs={{16,0},{32,16},{48,32},{64,48},{80,64},{96,80},{112,96},{128,112},... | collective-permute-start | bytes 393224 | tf_op jit(solution)/shard_map/while/body/eval_jaxpr/ppermute | solution.py:12
  322.2 12.8 %collective-permute-start = (bf16[16,4096]{1,0:T(8,128)(2,1)S(1)}, bf16[16,4096]{1,0:T(8,128)(2,1)S(1)}, u32[]{:S(2)}, u32[]{:S(2)}) collective-permute-start(bf16[16,4096]{1,0:T(8,128)(2,1)S(1)} %get-tuple-element.611), channel_id=1, source_target_pairs={{16,0},{32,16},{48,32},{64,48},{80,64},{96,80},{112,96},{128,112},... | collective-permute-start | bytes 393224 | tf_op jit(solution)/shard_map/while/body/eval_jaxpr/ppermute | solution.py:12
  335.1 13.3 %collective-permute-start = (bf16[16,4096]{1,0:T(8,128)(2,1)S(1)}, bf16[16,4096]{1,0:T(8,128)(2,1)S(1)}, u32[]{:S(2)}, u32[]{:S(2)}) collective-permute-start(bf16[16,4096]{1,0:T(8,128)(2,1)S(1)} %get-tuple-element.611), channel_id=1, source_target_pairs={{16,0},{32,16},{48,32},{64,48},{80,64},{96,80},{112,96},{128,112},... | collective-permute-start | bytes 393224 | tf_op jit(solution)/shard_map/while/body/eval_jaxpr/ppermute | solution.py:12
  348.4 12.7 %collective-permute-start = (bf16[16,4096]{1,0:T(8,128)(2,1)S(1)}, bf16[16,4096]{1,0:T(8,128)(2,1)S(1)}, u32[]{:S(2)}, u32[]{:S(2)}) collective-permute-start(bf16[16,4096]{1,0:T(8,128)(2,1)S(1)} %get-tuple-element.611), channel_id=1, source_target_pairs={{16,0},{32,16},{48,32},{64,48},{80,64},{96,80},{112,96},{128,112},... | collective-permute-start | bytes 393224 | tf_op jit(solution)/shard_map/while/body/eval_jaxpr/ppermute | solution.py:12
  361.1 12.3 %collective-permute-start = (bf16[16,4096]{1,0:T(8,128)(2,1)S(1)}, bf16[16,4096]{1,0:T(8,128)(2,1)S(1)}, u32[]{:S(2)}, u32[]{:S(2)}) collective-permute-start(bf16[16,4096]{1,0:T(8,128)(2,1)S(1)} %get-tuple-element.611), channel_id=1, source_target_pairs={{16,0},{32,16},{48,32},{64,48},{80,64},{96,80},{112,96},{128,112},... | collective-permute-start | bytes 393224 | tf_op jit(solution)/shard_map/while/body/eval_jaxpr/ppermute | solution.py:12
  373.4 12.3 %collective-permute-start = (bf16[16,4096]{1,0:T(8,128)(2,1)S(1)}, bf16[16,4096]{1,0:T(8,128)(2,1)S(1)}, u32[]{:S(2)}, u32[]{:S(2)}) collective-permute-start(bf16[16,4096]{1,0:T(8,128)(2,1)S(1)} %get-tuple-element.611), channel_id=1, source_target_pairs={{16,0},{32,16},{48,32},{64,48},{80,64},{96,80},{112,96},{128,112},... | collective-permute-start | bytes 393224 | tf_op jit(solution)/shard_map/while/body/eval_jaxpr/ppermute | solution.py:12
  385.8 12.3 %collective-permute-start = (bf16[16,4096]{1,0:T(8,128)(2,1)S(1)}, bf16[16,4096]{1,0:T(8,128)(2,1)S(1)}, u32[]{:S(2)}, u32[]{:S(2)}) collective-permute-start(bf16[16,4096]{1,0:T(8,128)(2,1)S(1)} %get-tuple-element.611), channel_id=1, source_target_pairs={{16,0},{32,16},{48,32},{64,48},{80,64},{96,80},{112,96},{128,112},... | collective-permute-start | bytes 393224 | tf_op jit(solution)/shard_map/while/body/eval_jaxpr/ppermute | solution.py:12
  398.1 12.3 %collective-permute-start = (bf16[16,4096]{1,0:T(8,128)(2,1)S(1)}, bf16[16,4096]{1,0:T(8,128)(2,1)S(1)}, u32[]{:S(2)}, u32[]{:S(2)}) collective-permute-start(bf16[16,4096]{1,0:T(8,128)(2,1)S(1)} %get-tuple-element.611), channel_id=1, source_target_pairs={{16,0},{32,16},{48,32},{64,48},{80,64},{96,80},{112,96},{128,112},... | collective-permute-start | bytes 393224 | tf_op jit(solution)/shard_map/while/body/eval_jaxpr/ppermute | solution.py:12
  410.4 12.3 %collective-permute-start = (bf16[16,4096]{1,0:T(8,128)(2,1)S(1)}, bf16[16,4096]{1,0:T(8,128)(2,1)S(1)}, u32[]{:S(2)}, u32[]{:S(2)}) collective-permute-start(bf16[16,4096]{1,0:T(8,128)(2,1)S(1)} %get-tuple-element.611), channel_id=1, source_target_pairs={{16,0},{32,16},{48,32},{64,48},{80,64},{96,80},{112,96},{128,112},... | collective-permute-start | bytes 393224 | tf_op jit(solution)/shard_map/while/body/eval_jaxpr/ppermute | solution.py:12
  422.8 12.3 %collective-permute-start = (bf16[16,4096]{1,0:T(8,128)(2,1)S(1)}, bf16[16,4096]{1,0:T(8,128)(2,1)S(1)}, u32[]{:S(2)}, u32[]{:S(2)}) collective-permute-start(bf16[16,4096]{1,0:T(8,128)(2,1)S(1)} %get-tuple-element.611), channel_id=1, source_target_pairs={{16,0},{32,16},{48,32},{64,48},{80,64},{96,80},{112,96},{128,112},... | collective-permute-start | bytes 393224 | tf_op jit(solution)/shard_map/while/body/eval_jaxpr/ppermute | solution.py:12
  435.1 12.3 %collective-permute-start = (bf16[16,4096]{1,0:T(8,128)(2,1)S(1)}, bf16[16,4096]{1,0:T(8,128)(2,1)S(1)}, u32[]{:S(2)}, u32[]{:S(2)}) collective-permute-start(bf16[16,4096]{1,0:T(8,128)(2,1)S(1)} %get-tuple-element.611), channel_id=1, source_target_pairs={{16,0},{32,16},{48,32},{64,48},{80,64},{96,80},{112,96},{128,112},... | collective-permute-start | bytes 393224 | tf_op jit(solution)/shard_map/while/body/eval_jaxpr/ppermute | solution.py:12
  447.4 12.3 %collective-permute-start = (bf16[16,4096]{1,0:T(8,128)(2,1)S(1)}, bf16[16,4096]{1,0:T(8,128)(2,1)S(1)}, u32[]{:S(2)}, u32[]{:S(2)}) collective-permute-start(bf16[16,4096]{1,0:T(8,128)(2,1)S(1)} %get-tuple-element.611), channel_id=1, source_target_pairs={{16,0},{32,16},{48,32},{64,48},{80,64},{96,80},{112,96},{128,112},... | collective-permute-start | bytes 393224 | tf_op jit(solution)/shard_map/while/body/eval_jaxpr/ppermute | solution.py:12
  459.8 12.3 %collective-permute-start = (bf16[16,4096]{1,0:T(8,128)(2,1)S(1)}, bf16[16,4096]{1,0:T(8,128)(2,1)S(1)}, u32[]{:S(2)}, u32[]{:S(2)}) collective-permute-start(bf16[16,4096]{1,0:T(8,128)(2,1)S(1)} %get-tuple-element.611), channel_id=1, source_target_pairs={{16,0},{32,16},{48,32},{64,48},{80,64},{96,80},{112,96},{128,112},... | collective-permute-start | bytes 393224 | tf_op jit(solution)/shard_map/while/body/eval_jaxpr/ppermute | solution.py:12
  472.1 18.9 %collective-permute-start = (bf16[16,4096]{1,0:T(8,128)(2,1)S(1)}, bf16[16,4096]{1,0:T(8,128)(2,1)S(1)}, u32[]{:S(2)}, u32[]{:S(2)}) collective-permute-start(bf16[16,4096]{1,0:T(8,128)(2,1)S(1)} %get-tuple-element.611), channel_id=1, source_target_pairs={{16,0},{32,16},{48,32},{64,48},{80,64},{96,80},{112,96},{128,112},... | collective-permute-start | bytes 393224 | tf_op jit(solution)/shard_map/while/body/eval_jaxpr/ppermute | solution.py:12
  491.0 3.1 copy-start.1
  497.7 12.3 %collective-permute-start = (bf16[16,4096]{1,0:T(8,128)(2,1)S(1)}, bf16[16,4096]{1,0:T(8,128)(2,1)S(1)}, u32[]{:S(2)}, u32[]{:S(2)}) collective-permute-start(bf16[16,4096]{1,0:T(8,128)(2,1)S(1)} %get-tuple-element.611), channel_id=1, source_target_pairs={{16,0},{32,16},{48,32},{64,48},{80,64},{96,80},{112,96},{128,112},... | collective-permute-start | bytes 393224 | tf_op jit(solution)/shard_map/while/body/eval_jaxpr/ppermute | solution.py:12
  510.0 3.1 copy-start.1
  516.6 12.3 %collective-permute-start = (bf16[16,4096]{1,0:T(8,128)(2,1)S(1)}, bf16[16,4096]{1,0:T(8,128)(2,1)S(1)}, u32[]{:S(2)}, u32[]{:S(2)}) collective-permute-start(bf16[16,4096]{1,0:T(8,128)(2,1)S(1)} %get-tuple-element.611), channel_id=1, source_target_pairs={{16,0},{32,16},{48,32},{64,48},{80,64},{96,80},{112,96},{128,112},... | collective-permute-start | bytes 393224 | tf_op jit(solution)/shard_map/while/body/eval_jaxpr/ppermute | solution.py:12
  528.9 3.1 copy-start.1
  535.5 12.3 %collective-permute-start = (bf16[16,4096]{1,0:T(8,128)(2,1)S(1)}, bf16[16,4096]{1,0:T(8,128)(2,1)S(1)}, u32[]{:S(2)}, u32[]{:S(2)}) collective-permute-start(bf16[16,4096]{1,0:T(8,128)(2,1)S(1)} %get-tuple-element.611), channel_id=1, source_target_pairs={{16,0},{32,16},{48,32},{64,48},{80,64},{96,80},{112,96},{128,112},... | collective-permute-start | bytes 393224 | tf_op jit(solution)/shard_map/while/body/eval_jaxpr/ppermute | solution.py:12
  547.8 3.1 copy-start.1
  554.5 12.3 %collective-permute-start = (bf16[16,4096]{1,0:T(8,128)(2,1)S(1)}, bf16[16,4096]{1,0:T(8,128)(2,1)S(1)}, u32[]{:S(2)}, u32[]{:S(2)}) collective-permute-start(bf16[16,4096]{1,0:T(8,128)(2,1)S(1)} %get-tuple-element.611), channel_id=1, source_target_pairs={{16,0},{32,16},{48,32},{64,48},{80,64},{96,80},{112,96},{128,112},... | collective-permute-start | bytes 393224 | tf_op jit(solution)/shard_map/while/body/eval_jaxpr/ppermute | solution.py:12
  566.8 3.1 copy-start.1
  573.5 12.3 %collective-permute-start = (bf16[16,4096]{1,0:T(8,128)(2,1)S(1)}, bf16[16,4096]{1,0:T(8,128)(2,1)S(1)}, u32[]{:S(2)}, u32[]{:S(2)}) collective-permute-start(bf16[16,4096]{1,0:T(8,128)(2,1)S(1)} %get-tuple-element.611), channel_id=1, source_target_pairs={{16,0},{32,16},{48,32},{64,48},{80,64},{96,80},{112,96},{128,112},... | collective-permute-start | bytes 393224 | tf_op jit(solution)/shard_map/while/body/eval_jaxpr/ppermute | solution.py:12
  585.8 3.1 copy-start.1
  592.4 12.3 %collective-permute-start = (bf16[16,4096]{1,0:T(8,128)(2,1)S(1)}, bf16[16,4096]{1,0:T(8,128)(2,1)S(1)}, u32[]{:S(2)}, u32[]{:S(2)}) collective-permute-start(bf16[16,4096]{1,0:T(8,128)(2,1)S(1)} %get-tuple-element.611), channel_id=1, source_target_pairs={{16,0},{32,16},{48,32},{64,48},{80,64},{96,80},{112,96},{128,112},... | collective-permute-start | bytes 393224 | tf_op jit(solution)/shard_map/while/body/eval_jaxpr/ppermute | solution.py:12
  604.7 3.1 copy-start.1
  611.3 12.3 %collective-permute-start = (bf16[16,4096]{1,0:T(8,128)(2,1)S(1)}, bf16[16,4096]{1,0:T(8,128)(2,1)S(1)}, u32[]{:S(2)}, u32[]{:S(2)}) collective-permute-start(bf16[16,4096]{1,0:T(8,128)(2,1)S(1)} %get-tuple-element.611), channel_id=1, source_target_pairs={{16,0},{32,16},{48,32},{64,48},{80,64},{96,80},{112,96},{128,112},... | collective-permute-start | bytes 393224 | tf_op jit(solution)/shard_map/while/body/eval_jaxpr/ppermute | solution.py:12
  623.7 3.1 copy-start.1
  630.3 5.7 collective-permute-start
  636.0 12.3 %collective-permute-start = (bf16[16,4096]{1,0:T(8,128)(2,1)S(1)}, bf16[16,4096]{1,0:T(8,128)(2,1)S(1)}, u32[]{:S(2)}, u32[]{:S(2)}) collective-permute-start(bf16[16,4096]{1,0:T(8,128)(2,1)S(1)} %get-tuple-element.611), channel_id=1, source_target_pairs={{16,0},{32,16},{48,32},{64,48},{80,64},{96,80},{112,96},{128,112},... | collective-permute-start | bytes 393224 | tf_op jit(solution)/shard_map/while/body/eval_jaxpr/ppermute | solution.py:12
  648.4 12.3 %collective-permute-start = (bf16[16,4096]{1,0:T(8,128)(2,1)S(1)}, bf16[16,4096]{1,0:T(8,128)(2,1)S(1)}, u32[]{:S(2)}, u32[]{:S(2)}) collective-permute-start(bf16[16,4096]{1,0:T(8,128)(2,1)S(1)} %get-tuple-element.611), channel_id=1, source_target_pairs={{16,0},{32,16},{48,32},{64,48},{80,64},{96,80},{112,96},{128,112},... | collective-permute-start | bytes 393224 | tf_op jit(solution)/shard_map/while/body/eval_jaxpr/ppermute | solution.py:12
  660.7 12.3 %collective-permute-start = (bf16[16,4096]{1,0:T(8,128)(2,1)S(1)}, bf16[16,4096]{1,0:T(8,128)(2,1)S(1)}, u32[]{:S(2)}, u32[]{:S(2)}) collective-permute-start(bf16[16,4096]{1,0:T(8,128)(2,1)S(1)} %get-tuple-element.611), channel_id=1, source_target_pairs={{16,0},{32,16},{48,32},{64,48},{80,64},{96,80},{112,96},{128,112},... | collective-permute-start | bytes 393224 | tf_op jit(solution)/shard_map/while/body/eval_jaxpr/ppermute | solution.py:12
  673.0 12.3 %collective-permute-start = (bf16[16,4096]{1,0:T(8,128)(2,1)S(1)}, bf16[16,4096]{1,0:T(8,128)(2,1)S(1)}, u32[]{:S(2)}, u32[]{:S(2)}) collective-permute-start(bf16[16,4096]{1,0:T(8,128)(2,1)S(1)} %get-tuple-element.611), channel_id=1, source_target_pairs={{16,0},{32,16},{48,32},{64,48},{80,64},{96,80},{112,96},{128,112},... | collective-permute-start | bytes 393224 | tf_op jit(solution)/shard_map/while/body/eval_jaxpr/ppermute | solution.py:12
  685.4 12.3 %collective-permute-start = (bf16[16,4096]{1,0:T(8,128)(2,1)S(1)}, bf16[16,4096]{1,0:T(8,128)(2,1)S(1)}, u32[]{:S(2)}, u32[]{:S(2)}) collective-permute-start(bf16[16,4096]{1,0:T(8,128)(2,1)S(1)} %get-tuple-element.611), channel_id=1, source_target_pairs={{16,0},{32,16},{48,32},{64,48},{80,64},{96,80},{112,96},{128,112},... | collective-permute-start | bytes 393224 | tf_op jit(solution)/shard_map/while/body/eval_jaxpr/ppermute | solution.py:12
  697.7 12.3 %collective-permute-start = (bf16[16,4096]{1,0:T(8,128)(2,1)S(1)}, bf16[16,4096]{1,0:T(8,128)(2,1)S(1)}, u32[]{:S(2)}, u32[]{:S(2)}) collective-permute-start(bf16[16,4096]{1,0:T(8,128)(2,1)S(1)} %get-tuple-element.611), channel_id=1, source_target_pairs={{16,0},{32,16},{48,32},{64,48},{80,64},{96,80},{112,96},{128,112},... | collective-permute-start | bytes 393224 | tf_op jit(solution)/shard_map/while/body/eval_jaxpr/ppermute | solution.py:12
  710.0 12.3 %collective-permute-start = (bf16[16,4096]{1,0:T(8,128)(2,1)S(1)}, bf16[16,4096]{1,0:T(8,128)(2,1)S(1)}, u32[]{:S(2)}, u32[]{:S(2)}) collective-permute-start(bf16[16,4096]{1,0:T(8,128)(2,1)S(1)} %get-tuple-element.611), channel_id=1, source_target_pairs={{16,0},{32,16},{48,32},{64,48},{80,64},{96,80},{112,96},{128,112},... | collective-permute-start | bytes 393224 | tf_op jit(solution)/shard_map/while/body/eval_jaxpr/ppermute | solution.py:12
  722.4 12.3 %collective-permute-start = (bf16[16,4096]{1,0:T(8,128)(2,1)S(1)}, bf16[16,4096]{1,0:T(8,128)(2,1)S(1)}, u32[]{:S(2)}, u32[]{:S(2)}) collective-permute-start(bf16[16,4096]{1,0:T(8,128)(2,1)S(1)} %get-tuple-element.611), channel_id=1, source_target_pairs={{16,0},{32,16},{48,32},{64,48},{80,64},{96,80},{112,96},{128,112},... | collective-permute-start | bytes 393224 | tf_op jit(solution)/shard_map/while/body/eval_jaxpr/ppermute | solution.py:12
  734.7 12.3 %collective-permute-start = (bf16[16,4096]{1,0:T(8,128)(2,1)S(1)}, bf16[16,4096]{1,0:T(8,128)(2,1)S(1)}, u32[]{:S(2)}, u32[]{:S(2)}) collective-permute-start(bf16[16,4096]{1,0:T(8,128)(2,1)S(1)} %get-tuple-element.611), channel_id=1, source_target_pairs={{16,0},{32,16},{48,32},{64,48},{80,64},{96,80},{112,96},{128,112},... | collective-permute-start | bytes 393224 | tf_op jit(solution)/shard_map/while/body/eval_jaxpr/ppermute | solution.py:12
  747.0 12.3 %collective-permute-start = (bf16[16,4096]{1,0:T(8,128)(2,1)S(1)}, bf16[16,4096]{1,0:T(8,128)(2,1)S(1)}, u32[]{:S(2)}, u32[]{:S(2)}) collective-permute-start(bf16[16,4096]{1,0:T(8,128)(2,1)S(1)} %get-tuple-element.611), channel_id=1, source_target_pairs={{16,0},{32,16},{48,32},{64,48},{80,64},{96,80},{112,96},{128,112},... | collective-permute-start | bytes 393224 | tf_op jit(solution)/shard_map/while/body/eval_jaxpr/ppermute | solution.py:12
  759.4 12.3 %collective-permute-start = (bf16[16,4096]{1,0:T(8,128)(2,1)S(1)}, bf16[16,4096]{1,0:T(8,128)(2,1)S(1)}, u32[]{:S(2)}, u32[]{:S(2)}) collective-permute-start(bf16[16,4096]{1,0:T(8,128)(2,1)S(1)} %get-tuple-element.611), channel_id=1, source_target_pairs={{16,0},{32,16},{48,32},{64,48},{80,64},{96,80},{112,96},{128,112},... | collective-permute-start | bytes 393224 | tf_op jit(solution)/shard_map/while/body/eval_jaxpr/ppermute | solution.py:12
  771.7 12.3 %collective-permute-start = (bf16[16,4096]{1,0:T(8,128)(2,1)S(1)}, bf16[16,4096]{1,0:T(8,128)(2,1)S(1)}, u32[]{:S(2)}, u32[]{:S(2)}) collective-permute-start(bf16[16,4096]{1,0:T(8,128)(2,1)S(1)} %get-tuple-element.611), channel_id=1, source_target_pairs={{16,0},{32,16},{48,32},{64,48},{80,64},{96,80},{112,96},{128,112},... | collective-permute-start | bytes 393224 | tf_op jit(solution)/shard_map/while/body/eval_jaxpr/ppermute | solution.py:12
  784.0 12.3 %collective-permute-start = (bf16[16,4096]{1,0:T(8,128)(2,1)S(1)}, bf16[16,4096]{1,0:T(8,128)(2,1)S(1)}, u32[]{:S(2)}, u32[]{:S(2)}) collective-permute-start(bf16[16,4096]{1,0:T(8,128)(2,1)S(1)} %get-tuple-element.611), channel_id=1, source_target_pairs={{16,0},{32,16},{48,32},{64,48},{80,64},{96,80},{112,96},{128,112},... | collective-permute-start | bytes 393224 | tf_op jit(solution)/shard_map/while/body/eval_jaxpr/ppermute | solution.py:12
  799.1 1.2 copy-start.4
Sparse Core Ops, SparseCore 0:
  10.1 88.6 all-gather.10
  100.9 83.6 all-gather.6
  186.5 85.0 all-gather.12
  274.2 83.3 all-gather.8
  799.3 124.8 reduce-scatter.1
where the time goes:
time: 935 us; the launch traced here: 932 us
  waiting for transfers between devices  714 us (76%)
  starting transfers between devices  87.2 us (9%)
  blocking collectives  43.8 us (5%)
  other arithmetic  33.4 us (4%)
  matrix products  32.9 us (4%)
  between operations  13.8 us (1%)
    ppermute x39, waiting for transfers between devices, from_behind(): return lax.ppermute(block, axis, route)  379 us
    all_gather x1, waiting for transfers between devices, per_device(): lax.all_gather(up_proj[0], 'dp', axis=1, tiled=True)  87.1 us
    ppermute x39, starting transfers between devices, from_behind(): return lax.ppermute(block, axis, route)  87 us
    all_gather x1, waiting for transfers between devices, per_device(): lax.all_gather(down_proj[0], 'dp', axis=0, tiled=True)  87 us
    all_gather x1, waiting for transfers between devices, per_device(): lax.all_gather(readout_matrix, 'dp', axis=0, tiled=True)  80.8 us
    reduce_scatter x1, waiting for transfers between devices, per_device(): lax.psum_scatter(contract_rows(normed, latent_grads), 'dp', scatter_dimen...  77.1 us
    all_to_all x1, blocking collectives, per_device(): lax.all_to_all(cotangents, 'dp', split_axis=1, concat_axis=0, tiled=True)  43.8 us
    dot_general x16, matrix products, multiply_trailing_factor(): lax.dot_general(left, right, (((1,), (1,)), ((), ())), preferred_element_...  24.7 us
  transfers between devices with their start and end apart: 44, of which 43 were waited for; matrix products, arithmetic and copies ran while one was open for 7% of the time, Pallas kernels for 0%

commit v1 on v0

--- a/solution.py
+++ b/solution.py
@@ -4,6 +4,13 @@
 from jax.sharding import PartitionSpec as P
 
 EPSILON = 1e-05
+
+
+def all_by_exchange(x, axis, along):
+    count = lax.axis_size(axis)
+    blocks = jnp.stack([x for _ in range(count)])
+    blocks = lax.all_to_all(blocks, axis, split_axis=0, concat_axis=0)
+    return jnp.concatenate(blocks, axis=along)
 
 
 def from_behind(block, axis, distance):
@@ -49,7 +56,7 @@
     down_full, up_full, entire_readout_matrix = (
         lax.all_gather(down_proj[0], "dp", axis=0, tiled=True),
         lax.all_gather(up_proj[0], "dp", axis=1, tiled=True),
-        lax.all_gather(readout_matrix, "dp", axis=0, tiled=True),
+        all_by_exchange(readout_matrix, "dp", 0),
     )
     inputs = section_inputs[0]
     gain_row = norm_gain[0]

time: 935 us -> 851 us (0.910)
  waiting for transfers between devices: 714 us -> 623 us
    all_gather x1 -> x0, waiting for transfers between devices: 80.8 us -> none  [per_device(): lax.all_gather(readout_matrix, 'dp', axis=0, tiled=True)]
  transfers between devices with their start and end apart: 44 -> 44, of which waited for: 43 -> 42; matrix products, arithmetic and copies ran while one was open for 7% -> 8% of each run, Pallas kernels for 0% -> 0%
where the time goes in v1:
time: 851 us; the launch traced here: 849 us
  waiting for transfers between devices  623 us (73%)
  starting transfers between devices  94.6 us (11%)
  blocking collectives  43.9 us (5%)
  matrix products  32.6 us (4%)
  other arithmetic  31.5 us (4%)
  between operations  13.9 us (2%)
    ppermute x39, waiting for transfers between devices, from_behind(): return lax.ppermute(block, axis, route)  379 us
    ppermute x39, starting transfers between devices, from_behind(): return lax.ppermute(block, axis, route)  87 us
    all_gather x1, waiting for transfers between devices, per_device(): lax.all_gather(down_proj[0], 'dp', axis=0, tiled=True)  86.4 us
    all_gather x1, waiting for transfers between devices, per_device(): lax.all_gather(up_proj[0], 'dp', axis=1, tiled=True)  79.1 us
    reduce_scatter x1, waiting for transfers between devices, per_device(): lax.psum_scatter(contract_rows(normed, latent_grads), 'dp', scatter_dimen...  76.3 us
    all_to_all x1, blocking collectives, per_device(): lax.all_to_all(cotangents, 'dp', split_axis=1, concat_axis=0, tiled=True)  43.9 us
    dot_general x16, matrix products, multiply_trailing_factor(): lax.dot_general(left, right, (((1,), (1,)), ((), ())), preferred_element_...  24.7 us
  transfers between devices with their start and end apart: 44, of which 42 were waited for; matrix products, arithmetic and copies ran while one was open for 8% of the time, Pallas kernels for 0%

profile of v1, /device:TPU:448, one launch (start us, length us, event | category | flops | bytes accessed | tf_op | source)
XLA Modules:
  0.0 848.9 jit_solution(17135947919062615947)
XLA Ops:
  8.7 2.0 stack.2
  10.7 7.4 all-to-all-start
  18.6 86.4 %all-gather.8.cloned.1.call-done = bf16[1,4096,256]{2,1,0:T(8,128)(2,1)} async-done(((bf16[1,256,256]{2,1,0:T(8,128)(2,1)}), bf16[1,4096,256]{2,1,0:T(8,128)(2,1)}) %all-gather.8.cloned.1.call-update) | async-done | bytes 2097168 | tf_op jit(solution)/shard_map/all_gather | solution.py:57
  105.0 2.8 multiply_convert_fusion.1
  109.6 79.1 %all-gather.10.cloned.1.call-done = bf16[1,256,4096]{2,1,0:T(8,128)(2,1)} async-done(((bf16[1,256,256]{2,1,0:T(8,128)(2,1)}), bf16[1,256,4096]{2,1,0:T(8,128)(2,1)}) %all-gather.10.cloned.1.call-update) | async-done | bytes 2097168 | tf_op jit(solution)/shard_map/all_gather | solution.py:58
  192.2 521.3 %while.20 = (s32[]{:T(128)}, bf16[16,4096]{1,0:T(8,128)(2,1)S(1)}, bf16[8,16,4096]{2,1,0:T(8,128)(2,1)}, bf16[8,16,256]{2,1,0:T(8,128)(2,1)S(1)}, bf16[8,16,4096...) while((s32[]{:T(128)}, bf16[16,4096]{1,0:T(8,128)(2,1)S(1)}, ...), condition=%wide.region_7.8_spmd, body=%wide.region_3.7_spmd.sunk | while | flops 67805192 | bytes 15549357 | solution.py:143
  194.1 2.5 collective-permute-done
  196.7 3.8 collective-permute-start
  200.5 2.5 collective-permute-done
  203.0 3.8 collective-permute-start
  206.8 7.2 collective-permute-done
  216.0 10.5 %collective-permute-done = bf16[16,4096]{1,0:T(8,128)(2,1)S(1)} collective-permute-done((bf16[16,4096]{1,0:T(8,128)(2,1)S(1)}, bf16[16,4096]{1,0:T(8,128)(2,1)S(1)}, u32[]{:S(2)}, u32[]{:S(2)}) %collective-permute-start) | collective-permute-done | bytes 131104 | tf_op jit(solution)/shard_map/while/body/eval_jaxpr/ppermute | solution.py:19
  226.5 1.9 collective-permute-start
  228.4 10.9 %collective-permute-done = bf16[16,4096]{1,0:T(8,128)(2,1)S(1)} collective-permute-done((bf16[16,4096]{1,0:T(8,128)(2,1)S(1)}, bf16[16,4096]{1,0:T(8,128)(2,1)S(1)}, u32[]{:S(2)}, u32[]{:S(2)}) %collective-permute-start) | collective-permute-done | bytes 131104 | tf_op jit(solution)/shard_map/while/body/eval_jaxpr/ppermute | solution.py:19
  241.3 11.0 %collective-permute-done = bf16[16,4096]{1,0:T(8,128)(2,1)S(1)} collective-permute-done((bf16[16,4096]{1,0:T(8,128)(2,1)S(1)}, bf16[16,4096]{1,0:T(8,128)(2,1)S(1)}, u32[]{:S(2)}, u32[]{:S(2)}) %collective-permute-start) | collective-permute-done | bytes 131104 | tf_op jit(solution)/shard_map/while/body/eval_jaxpr/ppermute | solution.py:19
  254.3 11.1 %collective-permute-done = bf16[16,4096]{1,0:T(8,128)(2,1)S(1)} collective-permute-done((bf16[16,4096]{1,0:T(8,128)(2,1)S(1)}, bf16[16,4096]{1,0:T(8,128)(2,1)S(1)}, u32[]{:S(2)}, u32[]{:S(2)}) %collective-permute-start) | collective-permute-done | bytes 131104 | tf_op jit(solution)/shard_map/while/body/eval_jaxpr/ppermute | solution.py:19
  267.4 10.7 %collective-permute-done = bf16[16,4096]{1,0:T(8,128)(2,1)S(1)} collective-permute-done((bf16[16,4096]{1,0:T(8,128)(2,1)S(1)}, bf16[16,4096]{1,0:T(8,128)(2,1)S(1)}, u32[]{:S(2)}, u32[]{:S(2)}) %collective-permute-start) | collective-permute-done | bytes 131104 | tf_op jit(solution)/shard_map/while/body/eval_jaxpr/ppermute | solution.py:19
  280.1 10.4 %collective-permute-done = bf16[16,4096]{1,0:T(8,128)(2,1)S(1)} collective-permute-done((bf16[16,4096]{1,0:T(8,128)(2,1)S(1)}, bf16[16,4096]{1,0:T(8,128)(2,1)S(1)}, u32[]{:S(2)}, u32[]{:S(2)}) %collective-permute-start) | collective-permute-done | bytes 131104 | tf_op jit(solution)/shard_map/while/body/eval_jaxpr/ppermute | solution.py:19
  292.5 10.4 %collective-permute-done = bf16[16,4096]{1,0:T(8,128)(2,1)S(1)} collective-permute-done((bf16[16,4096]{1,0:T(8,128)(2,1)S(1)}, bf16[16,4096]{1,0:T(8,128)(2,1)S(1)}, u32[]{:S(2)}, u32[]{:S(2)}) %collective-permute-start) | collective-permute-done | bytes 131104 | tf_op jit(solution)/shard_map/while/body/eval_jaxpr/ppermute | solution.py:19
  304.8 10.4 %collective-permute-done = bf16[16,4096]{1,0:T(8,128)(2,1)S(1)} collective-permute-done((bf16[16,4096]{1,0:T(8,128)(2,1)S(1)}, bf16[16,4096]{1,0:T(8,128)(2,1)S(1)}, u32[]{:S(2)}, u32[]{:S(2)}) %collective-permute-start) | collective-permute-done | bytes 131104 | tf_op jit(solution)/shard_map/while/body/eval_jaxpr/ppermute | solution.py:19
  317.1 10.4 %collective-permute-done = bf16[16,4096]{1,0:T(8,128)(2,1)S(1)} collective-permute-done((bf16[16,4096]{1,0:T(8,128)(2,1)S(1)}, bf16[16,4096]{1,0:T(8,128)(2,1)S(1)}, u32[]{:S(2)}, u32[]{:S(2)}) %collective-permute-start) | collective-permute-done | bytes 131104 | tf_op jit(solution)/shard_map/while/body/eval_jaxpr/ppermute | solution.py:19
  327.5 1.9 collective-permute-start
  329.5 10.4 %collective-permute-done = bf16[16,4096]{1,0:T(8,128)(2,1)S(1)} collective-permute-done((bf16[16,4096]{1,0:T(8,128)(2,1)S(1)}, bf16[16,4096]{1,0:T(8,128)(2,1)S(1)}, u32[]{:S(2)}, u32[]{:S(2)}) %collective-permute-start) | collective-permute-done | bytes 131104 | tf_op jit(solution)/shard_map/while/body/eval_jaxpr/ppermute | solution.py:19
  339.9 1.9 collective-permute-start
  341.8 10.4 %collective-permute-done = bf16[16,4096]{1,0:T(8,128)(2,1)S(1)} collective-permute-done((bf16[16,4096]{1,0:T(8,128)(2,1)S(1)}, bf16[16,4096]{1,0:T(8,128)(2,1)S(1)}, u32[]{:S(2)}, u32[]{:S(2)}) %collective-permute-start) | collective-permute-done | bytes 131104 | tf_op jit(solution)/shard_map/while/body/eval_jaxpr/ppermute | solution.py:19
  354.1 10.4 %collective-permute-done = bf16[16,4096]{1,0:T(8,128)(2,1)S(1)} collective-permute-done((bf16[16,4096]{1,0:T(8,128)(2,1)S(1)}, bf16[16,4096]{1,0:T(8,128)(2,1)S(1)}, u32[]{:S(2)}, u32[]{:S(2)}) %collective-permute-start) | collective-permute-done | bytes 131104 | tf_op jit(solution)/shard_map/while/body/eval_jaxpr/ppermute | solution.py:19
  366.5 10.4 %collective-permute-done = bf16[16,4096]{1,0:T(8,128)(2,1)S(1)} collective-permute-done((bf16[16,4096]{1,0:T(8,128)(2,1)S(1)}, bf16[16,4096]{1,0:T(8,128)(2,1)S(1)}, u32[]{:S(2)}, u32[]{:S(2)}) %collective-permute-start) | collective-permute-done | bytes 131104 | tf_op jit(solution)/shard_map/while/body/eval_jaxpr/ppermute | solution.py:19
  378.8 10.4 %collective-permute-done = bf16[16,4096]{1,0:T(8,128)(2,1)S(1)} collective-permute-done((bf16[16,4096]{1,0:T(8,128)(2,1)S(1)}, bf16[16,4096]{1,0:T(8,128)(2,1)S(1)}, u32[]{:S(2)}, u32[]{:S(2)}) %collective-permute-start) | collective-permute-done | bytes 131104 | tf_op jit(solution)/shard_map/while/body/eval_jaxpr/ppermute | solution.py:19
  391.1 17.0 %collective-permute-done = bf16[16,4096]{1,0:T(8,128)(2,1)S(1)} collective-permute-done((bf16[16,4096]{1,0:T(8,128)(2,1)S(1)}, bf16[16,4096]{1,0:T(8,128)(2,1)S(1)}, u32[]{:S(2)}, u32[]{:S(2)}) %collective-permute-start) | collective-permute-done | bytes 131104 | tf_op jit(solution)/shard_map/while/body/eval_jaxpr/ppermute | solution.py:19
  408.1 6.6 conditional.4
  416.7 10.4 %collective-permute-done = bf16[16,4096]{1,0:T(8,128)(2,1)S(1)} collective-permute-done((bf16[16,4096]{1,0:T(8,128)(2,1)S(1)}, bf16[16,4096]{1,0:T(8,128)(2,1)S(1)}, u32[]{:S(2)}, u32[]{:S(2)}) %collective-permute-start) | collective-permute-done | bytes 131104 | tf_op jit(solution)/shard_map/while/body/eval_jaxpr/ppermute | solution.py:19
  427.1 6.6 conditional.4
  435.6 10.4 %collective-permute-done = bf16[16,4096]{1,0:T(8,128)(2,1)S(1)} collective-permute-done((bf16[16,4096]{1,0:T(8,128)(2,1)S(1)}, bf16[16,4096]{1,0:T(8,128)(2,1)S(1)}, u32[]{:S(2)}, u32[]{:S(2)}) %collective-permute-start) | collective-permute-done | bytes 131104 | tf_op jit(solution)/shard_map/while/body/eval_jaxpr/ppermute | solution.py:19
  446.0 6.6 conditional.4
  454.6 10.3 %collective-permute-done = bf16[16,4096]{1,0:T(8,128)(2,1)S(1)} collective-permute-done((bf16[16,4096]{1,0:T(8,128)(2,1)S(1)}, bf16[16,4096]{1,0:T(8,128)(2,1)S(1)}, u32[]{:S(2)}, u32[]{:S(2)}) %collective-permute-start) | collective-permute-done | bytes 131104 | tf_op jit(solution)/shard_map/while/body/eval_jaxpr/ppermute | solution.py:19
  465.0 6.6 conditional.4
  473.5 10.4 %collective-permute-done = bf16[16,4096]{1,0:T(8,128)(2,1)S(1)} collective-permute-done((bf16[16,4096]{1,0:T(8,128)(2,1)S(1)}, bf16[16,4096]{1,0:T(8,128)(2,1)S(1)}, u32[]{:S(2)}, u32[]{:S(2)}) %collective-permute-start) | collective-permute-done | bytes 131104 | tf_op jit(solution)/shard_map/while/body/eval_jaxpr/ppermute | solution.py:19
  483.9 6.6 conditional.4
  492.5 10.4 %collective-permute-done = bf16[16,4096]{1,0:T(8,128)(2,1)S(1)} collective-permute-done((bf16[16,4096]{1,0:T(8,128)(2,1)S(1)}, bf16[16,4096]{1,0:T(8,128)(2,1)S(1)}, u32[]{:S(2)}, u32[]{:S(2)}) %collective-permute-start) | collective-permute-done | bytes 131104 | tf_op jit(solution)/shard_map/while/body/eval_jaxpr/ppermute | solution.py:19
  502.9 6.6 conditional.4
  511.5 10.3 %collective-permute-done = bf16[16,4096]{1,0:T(8,128)(2,1)S(1)} collective-permute-done((bf16[16,4096]{1,0:T(8,128)(2,1)S(1)}, bf16[16,4096]{1,0:T(8,128)(2,1)S(1)}, u32[]{:S(2)}, u32[]{:S(2)}) %collective-permute-start) | collective-permute-done | bytes 131104 | tf_op jit(solution)/shard_map/while/body/eval_jaxpr/ppermute | solution.py:19
  521.9 6.6 conditional.4
  530.4 10.4 %collective-permute-done = bf16[16,4096]{1,0:T(8,128)(2,1)S(1)} collective-permute-done((bf16[16,4096]{1,0:T(8,128)(2,1)S(1)}, bf16[16,4096]{1,0:T(8,128)(2,1)S(1)}, u32[]{:S(2)}, u32[]{:S(2)}) %collective-permute-start) | collective-permute-done | bytes 131104 | tf_op jit(solution)/shard_map/while/body/eval_jaxpr/ppermute | solution.py:19
  540.8 6.6 conditional.4
  549.4 3.7 collective-permute-done
  553.2 9.1 %collective-permute-start = (bf16[16,4096]{1,0:T(8,128)(2,1)S(1)}, bf16[16,4096]{1,0:T(8,128)(2,1)S(1)}, u32[]{:S(2)}, u32[]{:S(2)}) collective-permute-start(bf16[16,4096]{1,0:T(8,128)(2,1)S(1)} %get-tuple-element.612), channel_id=1, source_target_pairs={{16,0},{32,16},{48,32},{64,48},{80,64},{96,80},{112,96},{128,112},... | collective-permute-start | bytes 393224 | tf_op jit(solution)/shard_map/while/body/eval_jaxpr/ppermute | solution.py:19
  562.3 3.1 collective-permute-done
  565.5 3.1 collective-permute-start
  568.6 9.2 %collective-permute-done = bf16[16,4096]{1,0:T(8,128)(2,1)S(1)} collective-permute-done((bf16[16,4096]{1,0:T(8,128)(2,1)S(1)}, bf16[16,4096]{1,0:T(8,128)(2,1)S(1)}, u32[]{:S(2)}, u32[]{:S(2)}) %collective-permute-start) | collective-permute-done | bytes 131104 | tf_op jit(solution)/shard_map/while/body/eval_jaxpr/ppermute | solution.py:19
  579.8 10.4 %collective-permute-done = bf16[16,4096]{1,0:T(8,128)(2,1)S(1)} collective-permute-done((bf16[16,4096]{1,0:T(8,128)(2,1)S(1)}, bf16[16,4096]{1,0:T(8,128)(2,1)S(1)}, u32[]{:S(2)}, u32[]{:S(2)}) %collective-permute-start) | collective-permute-done | bytes 131104 | tf_op jit(solution)/shard_map/while/body/eval_jaxpr/ppermute | solution.py:19
  592.1 10.4 %collective-permute-done = bf16[16,4096]{1,0:T(8,128)(2,1)S(1)} collective-permute-done((bf16[16,4096]{1,0:T(8,128)(2,1)S(1)}, bf16[16,4096]{1,0:T(8,128)(2,1)S(1)}, u32[]{:S(2)}, u32[]{:S(2)}) %collective-permute-start) | collective-permute-done | bytes 131104 | tf_op jit(solution)/shard_map/while/body/eval_jaxpr/ppermute | solution.py:19
  604.5 10.4 %collective-permute-done = bf16[16,4096]{1,0:T(8,128)(2,1)S(1)} collective-permute-done((bf16[16,4096]{1,0:T(8,128)(2,1)S(1)}, bf16[16,4096]{1,0:T(8,128)(2,1)S(1)}, u32[]{:S(2)}, u32[]{:S(2)}) %collective-permute-start) | collective-permute-done | bytes 131104 | tf_op jit(solution)/shard_map/while/body/eval_jaxpr/ppermute | solution.py:19
  616.8 10.4 %collective-permute-done = bf16[16,4096]{1,0:T(8,128)(2,1)S(1)} collective-permute-done((bf16[16,4096]{1,0:T(8,128)(2,1)S(1)}, bf16[16,4096]{1,0:T(8,128)(2,1)S(1)}, u32[]{:S(2)}, u32[]{:S(2)}) %collective-permute-start) | collective-permute-done | bytes 131104 | tf_op jit(solution)/shard_map/while/body/eval_jaxpr/ppermute | solution.py:19
  629.1 10.4 %collective-permute-done = bf16[16,4096]{1,0:T(8,128)(2,1)S(1)} collective-permute-done((bf16[16,4096]{1,0:T(8,128)(2,1)S(1)}, bf16[16,4096]{1,0:T(8,128)(2,1)S(1)}, u32[]{:S(2)}, u32[]{:S(2)}) %collective-permute-start) | collective-permute-done | bytes 131104 | tf_op jit(solution)/shard_map/while/body/eval_jaxpr/ppermute | solution.py:19
  641.5 10.4 %collective-permute-done = bf16[16,4096]{1,0:T(8,128)(2,1)S(1)} collective-permute-done((bf16[16,4096]{1,0:T(8,128)(2,1)S(1)}, bf16[16,4096]{1,0:T(8,128)(2,1)S(1)}, u32[]{:S(2)}, u32[]{:S(2)}) %collective-permute-start) | collective-permute-done | bytes 131104 | tf_op jit(solution)/shard_map/while/body/eval_jaxpr/ppermute | solution.py:19
  653.8 10.4 %collective-permute-done = bf16[16,4096]{1,0:T(8,128)(2,1)S(1)} collective-permute-done((bf16[16,4096]{1,0:T(8,128)(2,1)S(1)}, bf16[16,4096]{1,0:T(8,128)(2,1)S(1)}, u32[]{:S(2)}, u32[]{:S(2)}) %collective-permute-start) | collective-permute-done | bytes 131104 | tf_op jit(solution)/shard_map/while/body/eval_jaxpr/ppermute | solution.py:19
  666.1 10.4 %collective-permute-done = bf16[16,4096]{1,0:T(8,128)(2,1)S(1)} collective-permute-done((bf16[16,4096]{1,0:T(8,128)(2,1)S(1)}, bf16[16,4096]{1,0:T(8,128)(2,1)S(1)}, u32[]{:S(2)}, u32[]{:S(2)}) %collective-permute-start) | collective-permute-done | bytes 131104 | tf_op jit(solution)/shard_map/while/body/eval_jaxpr/ppermute | solution.py:19
  678.5 10.4 %collective-permute-done = bf16[16,4096]{1,0:T(8,128)(2,1)S(1)} collective-permute-done((bf16[16,4096]{1,0:T(8,128)(2,1)S(1)}, bf16[16,4096]{1,0:T(8,128)(2,1)S(1)}, u32[]{:S(2)}, u32[]{:S(2)}) %collective-permute-start) | collective-permute-done | bytes 131104 | tf_op jit(solution)/shard_map/while/body/eval_jaxpr/ppermute | solution.py:19
  690.8 10.4 %collective-permute-done = bf16[16,4096]{1,0:T(8,128)(2,1)S(1)} collective-permute-done((bf16[16,4096]{1,0:T(8,128)(2,1)S(1)}, bf16[16,4096]{1,0:T(8,128)(2,1)S(1)}, u32[]{:S(2)}, u32[]{:S(2)}) %collective-permute-start) | collective-permute-done | bytes 131104 | tf_op jit(solution)/shard_map/while/body/eval_jaxpr/ppermute | solution.py:19
  703.1 10.4 %collective-permute-done = bf16[16,4096]{1,0:T(8,128)(2,1)S(1)} collective-permute-done((bf16[16,4096]{1,0:T(8,128)(2,1)S(1)}, bf16[16,4096]{1,0:T(8,128)(2,1)S(1)}, u32[]{:S(2)}, u32[]{:S(2)}) %collective-permute-start) | collective-permute-done | bytes 131104 | tf_op jit(solution)/shard_map/while/body/eval_jaxpr/ppermute | solution.py:19
  713.5 2.8 fusion.22
  718.1 43.9 %all_to_all.24 = bf16[128,16,256]{2,0,1:T(8,128)(2,1)S(1)} all-to-all(bf16[128,16,256]{2,0,1:T(8,128)(2,1)S(1)} %copy.16), channel_id=1, replica_groups=mesh['section'=32,'dp'=16] {'dp'}, dimensions={1} | all-to-all | bytes 2097152 | tf_op jit(solution)/shard_map/all_to_all | solution.py:151
  762.0 2.4 fusion.20
  764.4 76.3 %reduce-scatter.2.cloned.1.call-done = f32[256,256]{1,0:T(8,128)} async-done(((f32[4096,256]{1,0:T(8,128)}), f32[256,256]{1,0:T(8,128)}) %reduce-scatter.2.cloned.1.call-update) | async-done | bytes 262160 | tf_op jit(solution)/shard_map/reduce_scatter | solution.py:147
  (215 shorter events, 126.2 us)
Async XLA Ops:
  7.2 11.0 %copy-start.6 = (bf16[1,4096]{1,0:T(2,128)(2,1)S(1)}, bf16[1,4096]{1,0:T(2,128)(2,1)}, u32[]{:S(2)}) copy-start(bf16[1,4096]{1,0:T(2,128)(2,1)} %param.14) | copy-start | bytes 24580
  7.2 11.1 %copy-start.2 = (bf16[1,128,4096]{2,1,0:T(8,128)(2,1)S(1)}, bf16[1,128,4096]{2,1,0:T(8,128)(2,1)}, u32[]{:S(2)}) copy-start(bf16[1,128,4096]{2,1,0:T(8,128)(2,1)} %param.13) | copy-start | bytes 3145732
  7.2 97.8 %all-gather.8.cloned.1.call-start = ((), (), s32[]{:S(2)}) async-start(), calls=%async_computation.5 | async-start | bytes 2228224 | tf_op jit(solution)/shard_map/all_gather | solution.py:57
  7.9 180.8 %all-gather.10.cloned.1.call-start = ((), (), s32[]{:S(2)}) async-start(), calls=%async_computation.6 | async-start | bytes 2228224 | tf_op jit(solution)/shard_map/all_gather | solution.py:58
  10.7 99.0 %all-to-all-start = ((bf16[16,256,128]{2,1,0:T(8,128)(2,1)}), bf16[16,256,128]{2,1,0:T(8,128)(2,1)S(1)}, u32[]{:S(2)}, u32[]{:S(2)}) async-start(bf16[16,256,128]{2,1,0:T(8,128)(2,1)} %stack.2), calls=%async_computation | async-start | bytes 2097152 | tf_op jit(solution)/shard_map/all_to_all | solution.py:12
  18.1 743.9 %all-gather.6.cloned.1.call-start = ((), (), s32[]{:S(2)}) async-start(), calls=%async_computation.4 | async-start | bytes 1114112 | tf_op jit(solution)/shard_map/all_gather | solution.py:150
  18.6 89.4 %copy-start.7 = (s32[8]{0:T(128)S(1)}, s32[8]{0:T(128)}, u32[]{:S(2)}) copy-start(s32[8]{0:T(128)} %param.19) | copy-start | bytes 100
  107.8 81.0 %copy-start.4 = (bf16[128,256]{1,0:T(8,128)(2,1)S(1)}, bf16[128,256]{1,0:T(8,128)(2,1)}, u32[]{:S(2)}) copy-start(bf16[128,256]{1,0:T(8,128)(2,1)} %get-tuple-element.491) | copy-start | bytes 196612
  107.8 81.0 %copy-start.5 = (f32[128,128]{1,0:T(8,128)S(1)}, f32[128,128]{1,0:T(8,128)}, u32[]{:S(2)}) copy-start(f32[128,128]{1,0:T(8,128)} %param.18) | copy-start | bytes 196612
  107.8 732.9 %reduce-scatter.2.cloned.1.call-start = ((), (), s32[]{:S(2)}) async-start(), calls=%async_computation.3 | async-start | bytes 4456448 | tf_op jit(solution)/shard_map/reduce_scatter | solution.py:147
  189.9 2.3 copy-start
  192.2 4.4 collective-permute-start
  196.7 6.3 collective-permute-start
  203.0 11.0 %collective-permute-start = (bf16[16,4096]{1,0:T(8,128)(2,1)S(1)}, bf16[16,4096]{1,0:T(8,128)(2,1)S(1)}, u32[]{:S(2)}, u32[]{:S(2)}) collective-permute-start(bf16[16,4096]{1,0:T(8,128)(2,1)S(1)} %get-tuple-element.612), channel_id=1, source_target_pairs={{16,0},{32,16},{48,32},{64,48},{80,64},{96,80},{112,96},{128,112},... | collective-permute-start | bytes 393224 | tf_op jit(solution)/shard_map/while/body/eval_jaxpr/ppermute | solution.py:19
  214.0 12.4 %collective-permute-start = (bf16[16,4096]{1,0:T(8,128)(2,1)S(1)}, bf16[16,4096]{1,0:T(8,128)(2,1)S(1)}, u32[]{:S(2)}, u32[]{:S(2)}) collective-permute-start(bf16[16,4096]{1,0:T(8,128)(2,1)S(1)} %get-tuple-element.612), channel_id=1, source_target_pairs={{16,0},{32,16},{48,32},{64,48},{80,64},{96,80},{112,96},{128,112},... | collective-permute-start | bytes 393224 | tf_op jit(solution)/shard_map/while/body/eval_jaxpr/ppermute | solution.py:19
  226.5 12.9 %collective-permute-start = (bf16[16,4096]{1,0:T(8,128)(2,1)S(1)}, bf16[16,4096]{1,0:T(8,128)(2,1)S(1)}, u32[]{:S(2)}, u32[]{:S(2)}) collective-permute-start(bf16[16,4096]{1,0:T(8,128)(2,1)S(1)} %get-tuple-element.612), channel_id=1, source_target_pairs={{16,0},{32,16},{48,32},{64,48},{80,64},{96,80},{112,96},{128,112},... | collective-permute-start | bytes 393224 | tf_op jit(solution)/shard_map/while/body/eval_jaxpr/ppermute | solution.py:19
  239.4 13.0 %collective-permute-start = (bf16[16,4096]{1,0:T(8,128)(2,1)S(1)}, bf16[16,4096]{1,0:T(8,128)(2,1)S(1)}, u32[]{:S(2)}, u32[]{:S(2)}) collective-permute-start(bf16[16,4096]{1,0:T(8,128)(2,1)S(1)} %get-tuple-element.612), channel_id=1, source_target_pairs={{16,0},{32,16},{48,32},{64,48},{80,64},{96,80},{112,96},{128,112},... | collective-permute-start | bytes 393224 | tf_op jit(solution)/shard_map/while/body/eval_jaxpr/ppermute | solution.py:19
  252.4 13.1 %collective-permute-start = (bf16[16,4096]{1,0:T(8,128)(2,1)S(1)}, bf16[16,4096]{1,0:T(8,128)(2,1)S(1)}, u32[]{:S(2)}, u32[]{:S(2)}) collective-permute-start(bf16[16,4096]{1,0:T(8,128)(2,1)S(1)} %get-tuple-element.612), channel_id=1, source_target_pairs={{16,0},{32,16},{48,32},{64,48},{80,64},{96,80},{112,96},{128,112},... | collective-permute-start | bytes 393224 | tf_op jit(solution)/shard_map/while/body/eval_jaxpr/ppermute | solution.py:19
  265.5 12.7 %collective-permute-start = (bf16[16,4096]{1,0:T(8,128)(2,1)S(1)}, bf16[16,4096]{1,0:T(8,128)(2,1)S(1)}, u32[]{:S(2)}, u32[]{:S(2)}) collective-permute-start(bf16[16,4096]{1,0:T(8,128)(2,1)S(1)} %get-tuple-element.612), channel_id=1, source_target_pairs={{16,0},{32,16},{48,32},{64,48},{80,64},{96,80},{112,96},{128,112},... | collective-permute-start | bytes 393224 | tf_op jit(solution)/shard_map/while/body/eval_jaxpr/ppermute | solution.py:19
  278.2 12.3 %collective-permute-start = (bf16[16,4096]{1,0:T(8,128)(2,1)S(1)}, bf16[16,4096]{1,0:T(8,128)(2,1)S(1)}, u32[]{:S(2)}, u32[]{:S(2)}) collective-permute-start(bf16[16,4096]{1,0:T(8,128)(2,1)S(1)} %get-tuple-element.612), channel_id=1, source_target_pairs={{16,0},{32,16},{48,32},{64,48},{80,64},{96,80},{112,96},{128,112},... | collective-permute-start | bytes 393224 | tf_op jit(solution)/shard_map/while/body/eval_jaxpr/ppermute | solution.py:19
  290.5 12.3 %collective-permute-start = (bf16[16,4096]{1,0:T(8,128)(2,1)S(1)}, bf16[16,4096]{1,0:T(8,128)(2,1)S(1)}, u32[]{:S(2)}, u32[]{:S(2)}) collective-permute-start(bf16[16,4096]{1,0:T(8,128)(2,1)S(1)} %get-tuple-element.612), channel_id=1, source_target_pairs={{16,0},{32,16},{48,32},{64,48},{80,64},{96,80},{112,96},{128,112},... | collective-permute-start | bytes 393224 | tf_op jit(solution)/shard_map/while/body/eval_jaxpr/ppermute | solution.py:19
  302.9 12.3 %collective-permute-start = (bf16[16,4096]{1,0:T(8,128)(2,1)S(1)}, bf16[16,4096]{1,0:T(8,128)(2,1)S(1)}, u32[]{:S(2)}, u32[]{:S(2)}) collective-permute-start(bf16[16,4096]{1,0:T(8,128)(2,1)S(1)} %get-tuple-element.612), channel_id=1, source_target_pairs={{16,0},{32,16},{48,32},{64,48},{80,64},{96,80},{112,96},{128,112},... | collective-permute-start | bytes 393224 | tf_op jit(solution)/shard_map/while/body/eval_jaxpr/ppermute | solution.py:19
  315.2 12.3 %collective-permute-start = (bf16[16,4096]{1,0:T(8,128)(2,1)S(1)}, bf16[16,4096]{1,0:T(8,128)(2,1)S(1)}, u32[]{:S(2)}, u32[]{:S(2)}) collective-permute-start(bf16[16,4096]{1,0:T(8,128)(2,1)S(1)} %get-tuple-element.612), channel_id=1, source_target_pairs={{16,0},{32,16},{48,32},{64,48},{80,64},{96,80},{112,96},{128,112},... | collective-permute-start | bytes 393224 | tf_op jit(solution)/shard_map/while/body/eval_jaxpr/ppermute | solution.py:19
  327.5 12.3 %collective-permute-start = (bf16[16,4096]{1,0:T(8,128)(2,1)S(1)}, bf16[16,4096]{1,0:T(8,128)(2,1)S(1)}, u32[]{:S(2)}, u32[]{:S(2)}) collective-permute-start(bf16[16,4096]{1,0:T(8,128)(2,1)S(1)} %get-tuple-element.612), channel_id=1, source_target_pairs={{16,0},{32,16},{48,32},{64,48},{80,64},{96,80},{112,96},{128,112},... | collective-permute-start | bytes 393224 | tf_op jit(solution)/shard_map/while/body/eval_jaxpr/ppermute | solution.py:19
  339.9 12.3 %collective-permute-start = (bf16[16,4096]{1,0:T(8,128)(2,1)S(1)}, bf16[16,4096]{1,0:T(8,128)(2,1)S(1)}, u32[]{:S(2)}, u32[]{:S(2)}) collective-permute-start(bf16[16,4096]{1,0:T(8,128)(2,1)S(1)} %get-tuple-element.612), channel_id=1, source_target_pairs={{16,0},{32,16},{48,32},{64,48},{80,64},{96,80},{112,96},{128,112},... | collective-permute-start | bytes 393224 | tf_op jit(solution)/shard_map/while/body/eval_jaxpr/ppermute | solution.py:19
  352.2 12.3 %collective-permute-start = (bf16[16,4096]{1,0:T(8,128)(2,1)S(1)}, bf16[16,4096]{1,0:T(8,128)(2,1)S(1)}, u32[]{:S(2)}, u32[]{:S(2)}) collective-permute-start(bf16[16,4096]{1,0:T(8,128)(2,1)S(1)} %get-tuple-element.612), channel_id=1, source_target_pairs={{16,0},{32,16},{48,32},{64,48},{80,64},{96,80},{112,96},{128,112},... | collective-permute-start | bytes 393224 | tf_op jit(solution)/shard_map/while/body/eval_jaxpr/ppermute | solution.py:19
  364.5 12.3 %collective-permute-start = (bf16[16,4096]{1,0:T(8,128)(2,1)S(1)}, bf16[16,4096]{1,0:T(8,128)(2,1)S(1)}, u32[]{:S(2)}, u32[]{:S(2)}) collective-permute-start(bf16[16,4096]{1,0:T(8,128)(2,1)S(1)} %get-tuple-element.612), channel_id=1, source_target_pairs={{16,0},{32,16},{48,32},{64,48},{80,64},{96,80},{112,96},{128,112},... | collective-permute-start | bytes 393224 | tf_op jit(solution)/shard_map/while/body/eval_jaxpr/ppermute | solution.py:19
  376.9 12.3 %collective-permute-start = (bf16[16,4096]{1,0:T(8,128)(2,1)S(1)}, bf16[16,4096]{1,0:T(8,128)(2,1)S(1)}, u32[]{:S(2)}, u32[]{:S(2)}) collective-permute-start(bf16[16,4096]{1,0:T(8,128)(2,1)S(1)} %get-tuple-element.612), channel_id=1, source_target_pairs={{16,0},{32,16},{48,32},{64,48},{80,64},{96,80},{112,96},{128,112},... | collective-permute-start | bytes 393224 | tf_op jit(solution)/shard_map/while/body/eval_jaxpr/ppermute | solution.py:19
  389.2 18.9 %collective-permute-start = (bf16[16,4096]{1,0:T(8,128)(2,1)S(1)}, bf16[16,4096]{1,0:T(8,128)(2,1)S(1)}, u32[]{:S(2)}, u32[]{:S(2)}) collective-permute-start(bf16[16,4096]{1,0:T(8,128)(2,1)S(1)} %get-tuple-element.612), channel_id=1, source_target_pairs={{16,0},{32,16},{48,32},{64,48},{80,64},{96,80},{112,96},{128,112},... | collective-permute-start | bytes 393224 | tf_op jit(solution)/shard_map/while/body/eval_jaxpr/ppermute | solution.py:19
  408.1 3.1 copy-start.1
  414.8 12.3 %collective-permute-start = (bf16[16,4096]{1,0:T(8,128)(2,1)S(1)}, bf16[16,4096]{1,0:T(8,128)(2,1)S(1)}, u32[]{:S(2)}, u32[]{:S(2)}) collective-permute-start(bf16[16,4096]{1,0:T(8,128)(2,1)S(1)} %get-tuple-element.612), channel_id=1, source_target_pairs={{16,0},{32,16},{48,32},{64,48},{80,64},{96,80},{112,96},{128,112},... | collective-permute-start | bytes 393224 | tf_op jit(solution)/shard_map/while/body/eval_jaxpr/ppermute | solution.py:19
  427.1 3.1 copy-start.1
  433.7 12.3 %collective-permute-start = (bf16[16,4096]{1,0:T(8,128)(2,1)S(1)}, bf16[16,4096]{1,0:T(8,128)(2,1)S(1)}, u32[]{:S(2)}, u32[]{:S(2)}) collective-permute-start(bf16[16,4096]{1,0:T(8,128)(2,1)S(1)} %get-tuple-element.612), channel_id=1, source_target_pairs={{16,0},{32,16},{48,32},{64,48},{80,64},{96,80},{112,96},{128,112},... | collective-permute-start | bytes 393224 | tf_op jit(solution)/shard_map/while/body/eval_jaxpr/ppermute | solution.py:19
  446.0 3.1 copy-start.1
  452.7 12.3 %collective-permute-start = (bf16[16,4096]{1,0:T(8,128)(2,1)S(1)}, bf16[16,4096]{1,0:T(8,128)(2,1)S(1)}, u32[]{:S(2)}, u32[]{:S(2)}) collective-permute-start(bf16[16,4096]{1,0:T(8,128)(2,1)S(1)} %get-tuple-element.612), channel_id=1, source_target_pairs={{16,0},{32,16},{48,32},{64,48},{80,64},{96,80},{112,96},{128,112},... | collective-permute-start | bytes 393224 | tf_op jit(solution)/shard_map/while/body/eval_jaxpr/ppermute | solution.py:19
  465.0 3.1 copy-start.1
  471.6 12.3 %collective-permute-start = (bf16[16,4096]{1,0:T(8,128)(2,1)S(1)}, bf16[16,4096]{1,0:T(8,128)(2,1)S(1)}, u32[]{:S(2)}, u32[]{:S(2)}) collective-permute-start(bf16[16,4096]{1,0:T(8,128)(2,1)S(1)} %get-tuple-element.612), channel_id=1, source_target_pairs={{16,0},{32,16},{48,32},{64,48},{80,64},{96,80},{112,96},{128,112},... | collective-permute-start | bytes 393224 | tf_op jit(solution)/shard_map/while/body/eval_jaxpr/ppermute | solution.py:19
  483.9 3.1 copy-start.1
  490.6 12.3 %collective-permute-start = (bf16[16,4096]{1,0:T(8,128)(2,1)S(1)}, bf16[16,4096]{1,0:T(8,128)(2,1)S(1)}, u32[]{:S(2)}, u32[]{:S(2)}) collective-permute-start(bf16[16,4096]{1,0:T(8,128)(2,1)S(1)} %get-tuple-element.612), channel_id=1, source_target_pairs={{16,0},{32,16},{48,32},{64,48},{80,64},{96,80},{112,96},{128,112},... | collective-permute-start | bytes 393224 | tf_op jit(solution)/shard_map/while/body/eval_jaxpr/ppermute | solution.py:19
  502.9 3.1 copy-start.1
  509.6 12.3 %collective-permute-start = (bf16[16,4096]{1,0:T(8,128)(2,1)S(1)}, bf16[16,4096]{1,0:T(8,128)(2,1)S(1)}, u32[]{:S(2)}, u32[]{:S(2)}) collective-permute-start(bf16[16,4096]{1,0:T(8,128)(2,1)S(1)} %get-tuple-element.612), channel_id=1, source_target_pairs={{16,0},{32,16},{48,32},{64,48},{80,64},{96,80},{112,96},{128,112},... | collective-permute-start | bytes 393224 | tf_op jit(solution)/shard_map/while/body/eval_jaxpr/ppermute | solution.py:19
  521.9 3.1 copy-start.1
  528.5 12.3 %collective-permute-start = (bf16[16,4096]{1,0:T(8,128)(2,1)S(1)}, bf16[16,4096]{1,0:T(8,128)(2,1)S(1)}, u32[]{:S(2)}, u32[]{:S(2)}) collective-permute-start(bf16[16,4096]{1,0:T(8,128)(2,1)S(1)} %get-tuple-element.612), channel_id=1, source_target_pairs={{16,0},{32,16},{48,32},{64,48},{80,64},{96,80},{112,96},{128,112},... | collective-permute-start | bytes 393224 | tf_op jit(solution)/shard_map/while/body/eval_jaxpr/ppermute | solution.py:19
  540.8 3.1 copy-start.1
  547.5 5.7 collective-permute-start
  553.2 12.3 %collective-permute-start = (bf16[16,4096]{1,0:T(8,128)(2,1)S(1)}, bf16[16,4096]{1,0:T(8,128)(2,1)S(1)}, u32[]{:S(2)}, u32[]{:S(2)}) collective-permute-start(bf16[16,4096]{1,0:T(8,128)(2,1)S(1)} %get-tuple-element.612), channel_id=1, source_target_pairs={{16,0},{32,16},{48,32},{64,48},{80,64},{96,80},{112,96},{128,112},... | collective-permute-start | bytes 393224 | tf_op jit(solution)/shard_map/while/body/eval_jaxpr/ppermute | solution.py:19
  565.5 12.3 %collective-permute-start = (bf16[16,4096]{1,0:T(8,128)(2,1)S(1)}, bf16[16,4096]{1,0:T(8,128)(2,1)S(1)}, u32[]{:S(2)}, u32[]{:S(2)}) collective-permute-start(bf16[16,4096]{1,0:T(8,128)(2,1)S(1)} %get-tuple-element.612), channel_id=1, source_target_pairs={{16,0},{32,16},{48,32},{64,48},{80,64},{96,80},{112,96},{128,112},... | collective-permute-start | bytes 393224 | tf_op jit(solution)/shard_map/while/body/eval_jaxpr/ppermute | solution.py:19
  577.8 12.3 %collective-permute-start = (bf16[16,4096]{1,0:T(8,128)(2,1)S(1)}, bf16[16,4096]{1,0:T(8,128)(2,1)S(1)}, u32[]{:S(2)}, u32[]{:S(2)}) collective-permute-start(bf16[16,4096]{1,0:T(8,128)(2,1)S(1)} %get-tuple-element.612), channel_id=1, source_target_pairs={{16,0},{32,16},{48,32},{64,48},{80,64},{96,80},{112,96},{128,112},... | collective-permute-start | bytes 393224 | tf_op jit(solution)/shard_map/while/body/eval_jaxpr/ppermute | solution.py:19
  590.2 12.3 %collective-permute-start = (bf16[16,4096]{1,0:T(8,128)(2,1)S(1)}, bf16[16,4096]{1,0:T(8,128)(2,1)S(1)}, u32[]{:S(2)}, u32[]{:S(2)}) collective-permute-start(bf16[16,4096]{1,0:T(8,128)(2,1)S(1)} %get-tuple-element.612), channel_id=1, source_target_pairs={{16,0},{32,16},{48,32},{64,48},{80,64},{96,80},{112,96},{128,112},... | collective-permute-start | bytes 393224 | tf_op jit(solution)/shard_map/while/body/eval_jaxpr/ppermute | solution.py:19
  602.5 12.3 %collective-permute-start = (bf16[16,4096]{1,0:T(8,128)(2,1)S(1)}, bf16[16,4096]{1,0:T(8,128)(2,1)S(1)}, u32[]{:S(2)}, u32[]{:S(2)}) collective-permute-start(bf16[16,4096]{1,0:T(8,128)(2,1)S(1)} %get-tuple-element.612), channel_id=1, source_target_pairs={{16,0},{32,16},{48,32},{64,48},{80,64},{96,80},{112,96},{128,112},... | collective-permute-start | bytes 393224 | tf_op jit(solution)/shard_map/while/body/eval_jaxpr/ppermute | solution.py:19
  614.8 12.3 %collective-permute-start = (bf16[16,4096]{1,0:T(8,128)(2,1)S(1)}, bf16[16,4096]{1,0:T(8,128)(2,1)S(1)}, u32[]{:S(2)}, u32[]{:S(2)}) collective-permute-start(bf16[16,4096]{1,0:T(8,128)(2,1)S(1)} %get-tuple-element.612), channel_id=1, source_target_pairs={{16,0},{32,16},{48,32},{64,48},{80,64},{96,80},{112,96},{128,112},... | collective-permute-start | bytes 393224 | tf_op jit(solution)/shard_map/while/body/eval_jaxpr/ppermute | solution.py:19
  627.2 12.3 %collective-permute-start = (bf16[16,4096]{1,0:T(8,128)(2,1)S(1)}, bf16[16,4096]{1,0:T(8,128)(2,1)S(1)}, u32[]{:S(2)}, u32[]{:S(2)}) collective-permute-start(bf16[16,4096]{1,0:T(8,128)(2,1)S(1)} %get-tuple-element.612), channel_id=1, source_target_pairs={{16,0},{32,16},{48,32},{64,48},{80,64},{96,80},{112,96},{128,112},... | collective-permute-start | bytes 393224 | tf_op jit(solution)/shard_map/while/body/eval_jaxpr/ppermute | solution.py:19
  639.5 12.3 %collective-permute-start = (bf16[16,4096]{1,0:T(8,128)(2,1)S(1)}, bf16[16,4096]{1,0:T(8,128)(2,1)S(1)}, u32[]{:S(2)}, u32[]{:S(2)}) collective-permute-start(bf16[16,4096]{1,0:T(8,128)(2,1)S(1)} %get-tuple-element.612), channel_id=1, source_target_pairs={{16,0},{32,16},{48,32},{64,48},{80,64},{96,80},{112,96},{128,112},... | collective-permute-start | bytes 393224 | tf_op jit(solution)/shard_map/while/body/eval_jaxpr/ppermute | solution.py:19
  651.9 12.3 %collective-permute-start = (bf16[16,4096]{1,0:T(8,128)(2,1)S(1)}, bf16[16,4096]{1,0:T(8,128)(2,1)S(1)}, u32[]{:S(2)}, u32[]{:S(2)}) collective-permute-start(bf16[16,4096]{1,0:T(8,128)(2,1)S(1)} %get-tuple-element.612), channel_id=1, source_target_pairs={{16,0},{32,16},{48,32},{64,48},{80,64},{96,80},{112,96},{128,112},... | collective-permute-start | bytes 393224 | tf_op jit(solution)/shard_map/while/body/eval_jaxpr/ppermute | solution.py:19
  664.2 12.3 %collective-permute-start = (bf16[16,4096]{1,0:T(8,128)(2,1)S(1)}, bf16[16,4096]{1,0:T(8,128)(2,1)S(1)}, u32[]{:S(2)}, u32[]{:S(2)}) collective-permute-start(bf16[16,4096]{1,0:T(8,128)(2,1)S(1)} %get-tuple-element.612), channel_id=1, source_target_pairs={{16,0},{32,16},{48,32},{64,48},{80,64},{96,80},{112,96},{128,112},... | collective-permute-start | bytes 393224 | tf_op jit(solution)/shard_map/while/body/eval_jaxpr/ppermute | solution.py:19
  676.5 12.3 %collective-permute-start = (bf16[16,4096]{1,0:T(8,128)(2,1)S(1)}, bf16[16,4096]{1,0:T(8,128)(2,1)S(1)}, u32[]{:S(2)}, u32[]{:S(2)}) collective-permute-start(bf16[16,4096]{1,0:T(8,128)(2,1)S(1)} %get-tuple-element.612), channel_id=1, source_target_pairs={{16,0},{32,16},{48,32},{64,48},{80,64},{96,80},{112,96},{128,112},... | collective-permute-start | bytes 393224 | tf_op jit(solution)/shard_map/while/body/eval_jaxpr/ppermute | solution.py:19
  688.9 12.3 %collective-permute-start = (bf16[16,4096]{1,0:T(8,128)(2,1)S(1)}, bf16[16,4096]{1,0:T(8,128)(2,1)S(1)}, u32[]{:S(2)}, u32[]{:S(2)}) collective-permute-start(bf16[16,4096]{1,0:T(8,128)(2,1)S(1)} %get-tuple-element.612), channel_id=1, source_target_pairs={{16,0},{32,16},{48,32},{64,48},{80,64},{96,80},{112,96},{128,112},... | collective-permute-start | bytes 393224 | tf_op jit(solution)/shard_map/while/body/eval_jaxpr/ppermute | solution.py:19
  701.2 12.3 %collective-permute-start = (bf16[16,4096]{1,0:T(8,128)(2,1)S(1)}, bf16[16,4096]{1,0:T(8,128)(2,1)S(1)}, u32[]{:S(2)}, u32[]{:S(2)}) collective-permute-start(bf16[16,4096]{1,0:T(8,128)(2,1)S(1)} %get-tuple-element.612), channel_id=1, source_target_pairs={{16,0},{32,16},{48,32},{64,48},{80,64},{96,80},{112,96},{128,112},... | collective-permute-start | bytes 393224 | tf_op jit(solution)/shard_map/while/body/eval_jaxpr/ppermute | solution.py:19
  716.3 1.2 copy-start.3
Sparse Core Ops, SparseCore 0:
  10.1 94.8 all-gather.7
  107.0 81.6 all-gather.9
  191.4 83.3 all-gather.5
  716.4 124.2 reduce-scatter.1
